TPU v7x, 32 devices: a whole 2x2x4 slice. The times are simulated.
32 devices in a mesh: cam: 4 (over y, x), dev: 8 (over z, core).
Axes of the slice: x: 2, y: 2, z: 4, core: 2. Of those that a mesh axis runs over, the one named last changes fastest.
Arguments:
- params: float32 [256, 59, 128], P('dev'), may hold values from -4 to 4
- moment_first: float32 [8, 4, 8, 59, 128], P('dev', 'cam'), may hold values from -3 to 3
- moment_second: float32 [8, 4, 8, 59, 128], P('dev', 'cam'), may hold values from 0.01 to 1
- cam_proj: float32 [8, 9, 59], P('cam'), may hold values from -0.75 to 0.75
- send_block: int32 [8, 8, 8, 2], P('cam', 'dev'), may hold values from 0 to 31
- tile_slot: int32 [8, 16, 8], P('cam', 'dev'), may hold values from 0 to 15, as said below
- tile_count: int32 [8, 16], P('cam', 'dev'), may hold values from 2 to 8, as said below
- targets: float32 [8, 16, 3, 256], P('cam', 'dev'), may hold values from 0 to 1
- split_block: int32 [8, 8], P('dev'), may hold values from 0 to 31, as said below
- split_live: int32 [8, 8], P('dev'), may hold values from 0 to 1, as said below
Outputs:
- images: float32 [8, 16, 3, 256], P('cam', 'dev')
- new_params: float32 [256, 59, 128], P('dev')
- new_first: float32 [8, 4, 8, 59, 128], P('dev', 'cam')
- new_second: float32 [8, 4, 8, 59, 128], P('dev', 'cam')
- children: float32 [64, 2, 59, 128], P('dev')
Inputs may be any that keep to these rules, and one draw needn't show every extreme that they name: `tile_count`: in every camera some tile has exactly 8 live entries. `tile_slot`: the entries of one tile's list are distinct; entries at positions from the tile's count on are not read. `split_block`: among an owner's entries where split_live is 1 the blocks are distinct. `split_live`: each row holds exactly 2 ones; in every draw some new owner has a one in every row.
All inputs are finite; a program needn't handle non-finite values.
Results may differ from a plain program's by a relative error of at most 0.0003.
Values sent between devices are 32-bit elements; how exact they have to be, the bound alone decides.
A program may use at most 64 MiB of HBM per device.

v0:
```python
import math

import jax
import jax.numpy as jnp
from jax import lax
from jax.sharding import PartitionSpec as P

TSIDE = 16


LOSS_WEIGHT = 256.0
RATE = 0.01
BETA_FIRST = 0.9
BETA_SECOND = 0.999
EPSILON = 1e-08
SHRINK = math.log(1.6)
PRECISE = lax.Precision.HIGHEST


def unpack(projected):
    centre = 0.5 * TSIDE
    spread = 0.375 * TSIDE
    mean_x = centre + spread * jnp.tanh(projected[:, 0])
    mean_y = centre + spread * jnp.tanh(projected[:, 1])
    conic_a = 0.02 + 0.1 * jax.nn.softplus(projected[:, 2])
    conic_c = 0.02 + 0.1 * jax.nn.softplus(projected[:, 4])
    conic_b = 0.9 * jnp.sqrt(conic_a * conic_c) * jnp.tanh(projected[:, 3])
    opacity = 0.99 * jax.nn.sigmoid(projected[:, 5] - 6.0)
    shape_part = jnp.stack([mean_x, mean_y, conic_a, conic_b, conic_c, opacity], axis=1)
    return jnp.concatenate([shape_part, jax.nn.sigmoid(projected[:, 6:9])], axis=1)


def project(params, matrix):
    projected = jnp.einsum("pf,bfs->bps", matrix, params, precision=PRECISE)
    return unpack(projected)


def footprint(features, active, grid_x, grid_y):
    off_x = grid_x[None, None, :] - features[:, 0, :, None]
    off_y = grid_y[None, None, :] - features[:, 1, :, None]
    exponent = 0.5 * (
        features[:, 2, :, None] * off_x * off_x
        + 2.0 * features[:, 3, :, None] * off_x * off_y
        + features[:, 4, :, None] * off_y * off_y
    )
    falloff = jnp.exp(-exponent) * active[:, None, None]
    alpha_term = features[:, 5, :, None] * falloff
    return (off_x, off_y, falloff, alpha_term)


def divide(parents):
    offset = 0.5 * jnp.exp(parents[:, 3:6] - 1.0)
    shrunk = parents[:, 3:6] - SHRINK
    remainder = parents[:, 6:]
    child_plus = jnp.concatenate([parents[:, 0:3] + offset, shrunk, remainder], axis=1)
    child_minus = jnp.concatenate([parents[:, 0:3] - offset, shrunk, remainder], axis=1)
    return jnp.stack([child_plus, child_minus], axis=1)


def render(received, slot_list, counts, grid_x, grid_y, strict):
    tile_rows = slot_list.shape[0]
    pixels = grid_x.shape[0]

    def advance(position, state_carry):
        transmit, colour = state_carry
        slot_ids = lax.dynamic_index_in_dim(slot_list, position, 1, keepdims=False)
        features = jnp.take(received, slot_ids, axis=0)
        active = (counts > position).astype(jnp.float32)
        unused_x, unused_y, unused_fall, alpha_term = footprint(features, active, grid_x, grid_y)
        log_keep = jnp.log1p(-alpha_term)
        log_before = jnp.einsum("st,dtp->dsp", strict, log_keep, precision=PRECISE)
        weights = alpha_term * transmit[:, None, :] * jnp.exp(log_before)
        colour = colour + jnp.einsum("dcs,dsp->dcp", features[:, 6:9], weights, precision=PRECISE)
        transmit = transmit * jnp.exp(jnp.sum(log_keep, axis=1))
        return (transmit, colour)

    start_state = (
        jnp.ones((tile_rows, pixels), jnp.float32),
        jnp.zeros((tile_rows, 3, pixels), jnp.float32),
    )
    return lax.fori_loop(0, jnp.max(counts), advance, start_state)[1]


def render_grad(received, slot_list, counts, colour, target, grid_x, grid_y, strict, inclusive):
    tile_rows = slot_list.shape[0]
    pixels = grid_x.shape[0]
    cotangent = LOSS_WEIGHT * (colour - target)
    total_shade = jnp.sum(cotangent * colour, axis=1)

    def advance(position, state_carry):
        transmit, shade_upto, grad_buffer = state_carry
        slot_ids = lax.dynamic_index_in_dim(slot_list, position, 1, keepdims=False)
        features = jnp.take(received, slot_ids, axis=0)
        active = (counts > position).astype(jnp.float32)
        off_x, off_y, falloff, alpha_term = footprint(features, active, grid_x, grid_y)
        log_keep = jnp.log1p(-alpha_term)
        log_before = jnp.einsum("st,dtp->dsp", strict, log_keep, precision=PRECISE)
        reach_here = transmit[:, None, :] * jnp.exp(log_before)
        weights = alpha_term * reach_here
        shade_dot = jnp.einsum("dcp,dcs->dsp", cotangent, features[:, 6:9], precision=PRECISE)
        shade_part = shade_dot * weights
        shade_after = (
            total_shade[:, None, :]
            - shade_upto[:, None, :]
            - jnp.einsum("st,dtp->dsp", inclusive, shade_part, precision=PRECISE)
        )
        d_alpha = reach_here * shade_dot - shade_after / (1.0 - alpha_term)
        pull_term = d_alpha * alpha_term
        conic_a = features[:, 2, :, None]
        conic_b = features[:, 3, :, None]
        conic_c = features[:, 4, :, None]
        shape_grads = jnp.stack(
            [
                jnp.sum(pull_term * (conic_a * off_x + conic_b * off_y), axis=2),
                jnp.sum(pull_term * (conic_b * off_x + conic_c * off_y), axis=2),
                -0.5 * jnp.sum(pull_term * off_x * off_x, axis=2),
                -jnp.sum(pull_term * off_x * off_y, axis=2),
                -0.5 * jnp.sum(pull_term * off_y * off_y, axis=2),
                jnp.sum(d_alpha * falloff, axis=2),
            ],
            axis=1,
        )
        colour_grads = jnp.einsum("dcp,dsp->dcs", cotangent, weights, precision=PRECISE)
        grad_piece = jnp.concatenate([shape_grads, colour_grads], axis=1)
        grad_buffer = grad_buffer.at[slot_ids].add(grad_piece)
        shade_upto = shade_upto + jnp.sum(shade_part, axis=1)
        transmit = transmit * jnp.exp(jnp.sum(log_keep, axis=1))
        return (transmit, shade_upto, grad_buffer)

    start_state = (
        jnp.ones((tile_rows, pixels), jnp.float32),
        jnp.zeros((tile_rows, pixels), jnp.float32),
        jnp.zeros(received.shape, jnp.float32),
    )
    return lax.fori_loop(0, jnp.max(counts), advance, start_state)[2]


def body(
    params,
    moment_first,
    moment_second,
    cam_proj,
    send_block,
    tile_slot,
    tile_count,
    targets,
    split_block,
    split_live,
):
    groups_here = cam_proj.shape[0]
    owned = params.shape[0]
    splats = params.shape[2]
    pixel_ids = jnp.arange(TSIDE * TSIDE, dtype=jnp.int32)
    grid_x = (pixel_ids % TSIDE).astype(jnp.float32) + 0.5
    grid_y = (pixel_ids // TSIDE).astype(jnp.float32) + 0.5
    splat_ids = jnp.arange(splats, dtype=jnp.int32)
    strict = (splat_ids[None, :] < splat_ids[:, None]).astype(jnp.float32)
    inclusive = (splat_ids[None, :] <= splat_ids[:, None]).astype(jnp.float32)
    block_ids = jnp.arange(owned, dtype=jnp.int32)
    outgoing = []
    pullbacks = []
    selectors = []
    for camera in range(groups_here):
        features, pullback = jax.vjp(lambda values: project(values, cam_proj[camera]), params)
        chosen_ids = send_block[camera, 0].reshape(-1)
        outgoing.append(jnp.take(features, chosen_ids, axis=0))
        pullbacks.append(pullback)
        selectors.append((chosen_ids[:, None] == block_ids[None, :]).astype(jnp.float32))
    images = []
    gradient = jnp.zeros(params.shape, jnp.float32)
    arrived = lax.all_to_all(jnp.stack(outgoing), "dev", split_axis=1, concat_axis=1, tiled=True)
    buffers = []
    for camera in range(groups_here):
        received = arrived[camera]
        colour = render(received, tile_slot[camera], tile_count[camera], grid_x, grid_y, strict)
        grad_buffer = render_grad(
            received,
            tile_slot[camera],
            tile_count[camera],
            colour,
            targets[camera],
            grid_x,
            grid_y,
            strict,
            inclusive,
        )
        colour, grad_buffer = (colour, grad_buffer)
        images.append(colour)
        buffers.append(grad_buffer)
    returned = lax.all_to_all(jnp.stack(buffers), "dev", split_axis=1, concat_axis=1, tiled=True)
    for camera in range(groups_here):
        owner_returned = returned[camera]
        per_block = jnp.einsum("nb,nps->bps", selectors[camera], owner_returned, precision=PRECISE)
        gradient = gradient + pullbacks[camera](per_block)[0]
    share_rows = owned // lax.axis_size("cam")
    first_row = lax.axis_index("cam") * share_rows
    summed_grad = lax.psum(gradient, "cam")
    grad_share = lax.dynamic_slice_in_dim(summed_grad, first_row, share_rows, 0)
    own_params = lax.dynamic_slice_in_dim(params, first_row, share_rows, 0)
    first_moment = moment_first.reshape(grad_share.shape)
    second_moment = moment_second.reshape(grad_share.shape)
    new_first = BETA_FIRST * first_moment + (1.0 - BETA_FIRST) * grad_share
    new_second = BETA_SECOND * second_moment + (1.0 - BETA_SECOND) * grad_share * grad_share
    new_share = own_params - RATE * new_first / (jnp.sqrt(new_second) + EPSILON)
    new_params = lax.all_gather(new_share, "cam", axis=0, tiled=True)
    split_ids = split_block[0]
    live_mask = split_live[0]
    parents = jnp.take(new_params, split_ids, axis=0) * live_mask.astype(jnp.float32)[:, None, None]
    outgoing_children = divide(parents) * live_mask.astype(jnp.float32)[:, None, None, None]
    children = lax.all_to_all(outgoing_children, "dev", split_axis=0, concat_axis=0, tiled=True)
    return (
        jnp.stack(images),
        new_params,
        new_first.reshape(moment_first.shape),
        new_second.reshape(moment_second.shape),
        children,
    )


def solution(mesh):
    placed = (
        P("dev", None, None),
        P("dev", "cam", None, None, None),
        P("dev", "cam", None, None, None),
        P("cam", None, None),
        P("cam", "dev", None, None),
        P("cam", "dev", None),
        P("cam", "dev"),
        P("cam", "dev", None, None),
        P("dev", None),
        P("dev", None),
    )
    return jax.shard_map(
        body,
        mesh=mesh,
        in_specs=placed,
        out_specs=(
            P("cam", "dev", None, None),
            P("dev", None, None),
            P("dev", "cam", None, None, None),
            P("dev", "cam", None, None, None),
            P("dev", None, None, None),
        ),
        check_vma=False,
    )
```

profile of v0, /device:TPU:1, one launch (start us, length us, event | category | flops | bytes accessed | tf_op | source)
XLA Modules:
  0.0 274.1 jit_solution(13150151495697877418)
XLA Ops:
  7.2 0.7 fusion.241
  8.7 2.5 fusion.223
  11.6 1.2 fusion.222
  14.5 0.8 copy.472
  15.3 6.5 %all-to-all-start = ((f32[2,16,9,128]{3,0,2,1:T(2,128)}), f32[2,16,9,128]{3,0,2,1:T(2,128)S(1)}, u32[]{:S(2)}, u32[]{:S(2)}) async-start(f32[2,16,9,128]{3,0,2,1:T(2,128)} %copy.472), calls=%async_computation | async-start | bytes 294912 | tf_op jit(solution)/shard_map/all_to_all | solution.py:171
  21.8 0.7 copy-done.6
  22.5 0.6 slice_bitcast_fusion.13
  23.3 4.5 %all-to-all-done = f32[2,16,9,128]{3,0,2,1:T(2,128)S(1)} async-done(((f32[2,16,9,128]{3,0,2,1:T(2,128)}), f32[2,16,9,128]{3,0,2,1:T(2,128)S(1)}, u32[]{:S(2)}, u32[]{:S(2)}) %all-to-all-start) | async-done | bytes 147488 | tf_op jit(solution)/shard_map/all_to_all | solution.py:171
  27.9 14.1 %while.56 = (s32[]{:T(128)}, f32[2,256]{1,0:T(2,128)S(1)}, f32[2,3,256]{2,1,0:T(4,128)S(1)}, s32[]{:T(128)}, s32[2,8]{0,1:T(8,128)S(1)}, /*index=5*/f32[16,9,128...) while((s32[]{:T(128)}, f32[2,256]{1,0:T(2,128)S(1)}, ...), condition=%wide.region_3.7_spmd.clone, body=%wide.region_1.6_spmd.clone.sunk | while | flops 106144784 | bytes 624851 | solution.py:81
  42.1 26.8 %while.58 = (s32[]{:T(128)}, f32[2,256]{1,0:T(2,128)S(1)}, f32[2,256]{1,0:T(2,128)S(1)}, f32[16,9,128]{2,1,0:T(8,128)S(1)}, s32[]{:T(128)}, /*index=5*/s32[2,8]{...) while((s32[]{:T(128)}, f32[2,256]{1,0:T(2,128)S(1)}, ...), condition=%wide.region_19.23_spmd.clone, body=%wide.region_9.22_spmd.clone.sunk | while | flops 212018704 | bytes 1500431 | solution.py:135
  43.5 0.7 fusion.303
  45.3 1.3 fusion.304
  48.7 0.7 fusion.303
  50.5 1.3 fusion.304
  53.9 0.7 fusion.303
  55.7 1.3 fusion.304
  59.2 0.7 fusion.303
  60.9 1.3 fusion.304
  64.4 0.7 fusion.303
  66.2 1.2 fusion.304
  69.0 16.8 %while.57 = (s32[]{:T(128)}, f32[2,256]{1,0:T(2,128)S(1)}, f32[2,3,256]{2,1,0:T(4,128)S(1)}, s32[]{:T(128)}, s32[2,8]{0,1:T(8,128)S(1)}, /*index=5*/f32[16,9,128...) while((s32[]{:T(128)}, f32[2,256]{1,0:T(2,128)S(1)}, ...), condition=%wide.region_7.11_spmd.clone, body=%wide.region_5.10_spmd.clone.sunk | while | flops 106144784 | bytes 624851 | solution.py:81
  85.8 32.0 %while.59 = (s32[]{:T(128)}, f32[2,256]{1,0:T(2,128)S(1)}, f32[2,256]{1,0:T(2,128)S(1)}, f32[16,9,128]{2,1,0:T(8,128)S(1)}, s32[]{:T(128)}, /*index=5*/s32[2,8]{...) while((s32[]{:T(128)}, f32[2,256]{1,0:T(2,128)S(1)}, ...), condition=%wide.region_31.35_spmd.clone, body=%wide.region_21.34_spmd.clone.sunk | while | flops 212018704 | bytes 1500431 | solution.py:135
  87.2 0.7 fusion.313
  89.0 1.2 fusion.314
  92.4 0.7 fusion.313
  94.2 1.2 fusion.314
  97.7 0.7 fusion.313
  99.4 1.2 fusion.314
  102.9 0.7 fusion.313
  104.7 1.2 fusion.314
  108.1 0.7 fusion.313
  109.9 1.2 fusion.314
  113.3 0.7 fusion.313
  115.1 1.2 fusion.314
  118.0 49.0 %all_to_all.15 = f32[2,16,9,128]{3,0,2,1:T(2,128)S(1)} all-to-all(f32[2,16,9,128]{3,0,2,1:T(2,128)S(1)} %copy.491), channel_id=1, replica_groups=mesh['cam'=4,'dev'=8] {'dev'}, dimensions={1} | all-to-all | bytes 294912 | tf_op jit(solution)/shard_map/all_to_all | solution.py:190
  168.1 1.0 fusion.151
  169.1 2.1 fusion.148
  171.8 0.6 copy-done.7
  173.2 49.4 %all-reduce.16.cloned.1.call-done = f32[32,59,128]{2,1,0:T(8,128)} async-done(((f32[32,59,128]{2,1,0:T(8,128)}), f32[32,59,128]{2,1,0:T(8,128)}) %all-reduce.16.cloned.1.call-update) | async-done | bytes 966672 | tf_op jit(solution)/shard_map/psum | solution.py:197
  222.5 1.2 fusion.169
  223.9 18.8 %all_gather.3 = f32[32,59,128]{2,0,1:T(8,128)S(1)} all-gather(f32[8,59,128]{2,0,1:T(8,128)S(1)} %copy.497), channel_id=1, replica_groups=mesh['cam'=4,'dev'=8] {'cam'}, dimensions={0}, use_global_device_ids=true | all-gather | bytes 1208320 | tf_op jit(solution)/shard_map/all_gather | solution.py:205
  244.1 1.0 copy.500
  245.2 6.9 %all-to-all-start.2 = ((f32[8,2,59,128]{3,1,2,0:T(2,128)}), f32[8,2,59,128]{3,1,2,0:T(2,128)S(1)}, u32[]{:S(2)}, u32[]{:S(2)}) async-start(f32[8,2,59,128]{3,1,2,0:T(2,128)} %copy.500), calls=%async_computation.2 | async-start | bytes 966656 | tf_op jit(solution)/shard_map/all_to_all | solution.py:210
  252.7 0.8 copy.501
  253.5 0.8 copy.502
  254.3 11.2 %all-to-all-done.2 = f32[8,2,59,128]{3,1,2,0:T(2,128)S(1)} async-done(((f32[8,2,59,128]{3,1,2,0:T(2,128)}), f32[8,2,59,128]{3,1,2,0:T(2,128)S(1)}, u32[]{:S(2)}, u32[]{:S(2)}) %all-to-all-start.2) | async-done | bytes 483360 | tf_op jit(solution)/shard_map/all_to_all | solution.py:210
  265.5 0.9 copy.647
  266.5 0.8 copy.648
  (408 shorter events, 56.5 us)
Async XLA Ops:
  7.9 0.7 copy-start.4
  8.7 2.9 %copy-start = (f32[32,59,128]{2,0,1:T(8,128)S(1)}, f32[32,59,128]{2,0,1:T(8,128)}, u32[]{:S(2)}) copy-start(f32[32,59,128]{2,0,1:T(8,128)} %param.23) | copy-start | bytes 2899972
  15.3 6.5 %copy-start.5 = (s32[2,2,8]{2,1,0:T(2,128)S(1)}, s32[2,2,8]{2,1,0:T(2,128)}, u32[]{:S(2)}) copy-start(s32[2,2,8]{2,1,0:T(2,128)} %param.28) | copy-start | bytes 388
  15.3 12.5 %all-to-all-start = ((f32[2,16,9,128]{3,0,2,1:T(2,128)}), f32[2,16,9,128]{3,0,2,1:T(2,128)S(1)}, u32[]{:S(2)}, u32[]{:S(2)}) async-start(f32[2,16,9,128]{3,0,2,1:T(2,128)} %copy.472), calls=%async_computation | async-start | bytes 294912 | tf_op jit(solution)/shard_map/all_to_all | solution.py:171
  21.8 0.7 copy-start.6
  21.8 200.7 %all-reduce.16.cloned.1.call-start = ((), (), s32[]{:S(2)}) async-start(), calls=%async_computation.3 | async-start | bytes 2097152 | tf_op jit(solution)/shard_map/psum | solution.py:197
  22.5 0.8 copy-start.3
  171.2 51.3 %copy-start.1 = (f32[1,1,8,59,128]{4,2,3,1,0:T(8,128)S(1)}, f32[1,1,8,59,128]{4,2,3,1,0:T(8,128)}, u32[]{:S(2)}) copy-start(f32[1,1,8,59,128]{4,2,3,1,0:T(8,128)} %param.25) | copy-start | bytes 724996
  171.2 51.3 %copy-start.2 = (f32[1,1,8,59,128]{4,2,3,1,0:T(8,128)S(1)}, f32[1,1,8,59,128]{4,2,3,1,0:T(8,128)}, u32[]{:S(2)}) copy-start(f32[1,1,8,59,128]{4,2,3,1,0:T(8,128)} %param.24) | copy-start | bytes 724996
  171.8 0.7 copy-start.7
  172.5 0.7 copy-start.8
  245.2 20.4 %all-to-all-start.2 = ((f32[8,2,59,128]{3,1,2,0:T(2,128)}), f32[8,2,59,128]{3,1,2,0:T(2,128)S(1)}, u32[]{:S(2)}, u32[]{:S(2)}) async-start(f32[8,2,59,128]{3,1,2,0:T(2,128)} %copy.500), calls=%async_computation.2 | async-start | bytes 966656 | tf_op jit(solution)/shard_map/all_to_all | solution.py:210
Sparse Core Ops, SparseCore 0:
  171.4 51.1 all-reduce.15
where the time goes:
time: 276 us; the launch traced here: 274 us
  blocking collectives  67.8 us (25%)
  waiting for transfers between devices  65.1 us (24%)
  matrix products  50.8 us (18%)
  local copies, waits for them, and re-layouts  26 us (9%)
  loops' own time  19.2 us (7%)
  other arithmetic  17.4 us (6%)
  between operations  14.6 us (5%)
  starting transfers between devices  13.4 us (5%)
    psum x1, waiting for transfers between devices, body(): summed_grad = lax.psum(gradient, 'cam')  49.4 us
    all_to_all x1, blocking collectives, body(): lax.all_to_all(jnp.stack(buffers), 'dev', split_axis=1, concat_axis=1, ti...  49 us
    all_gather x1, blocking collectives, body(): new_params = lax.all_gather(new_share, 'cam', axis=0, tiled=True)  18.8 us
    dot_general x22, matrix products, advance(): log_before = jnp.einsum('st,dtp->dsp', strict, log_keep, precision=PRECISE)  14.7 us
    dot_general x11, matrix products, advance(): jnp.einsum('st,dtp->dsp', inclusive, shade_part, precision=PRECISE)  13.8 us
    gather x22, local copies, waits for them, and re-layouts, advance(): features = jnp.take(received, slot_ids, axis=0)  12.1 us
    all_to_all x1, waiting for transfers between devices, body(): lax.all_to_all(outgoing_children, 'dev', split_axis=0, concat_axis=0, til...  11.2 us
    another operation x2, loops' own time, render_grad(): return lax.fori_loop(0, jnp.max(counts), advance, start_state)[2]  9.95 us
  transfers between devices with their start and end apart: 3, of which 3 were waited for; matrix products, arithmetic and copies ran while one was open for 1% of the time, Pallas kernels for 0%

commit v1 on v0

v1 whole, which is shorter than its diff:
```python
import functools
import math

import jax
import jax.numpy as jnp
from jax import lax
from jax.experimental import pallas as pl
from jax.experimental.pallas import tpu as pltpu
from jax.sharding import PartitionSpec as P

TSIDE = 16
PROJ = 9
LOSS_WEIGHT = 256.0
RATE = 0.01
BETA_FIRST = 0.9
BETA_SECOND = 0.999
EPSILON = 1e-08
SHRINK = math.log(1.6)
LOG2E = math.log2(math.e)
MESH = pl.DeviceIdType.MESH
HIGHEST = lax.Precision.HIGHEST
F32 = jnp.float32
BF16 = jnp.bfloat16
VMEM = pl.BlockSpec(memory_space=pltpu.VMEM)
SMEM = pl.BlockSpec(memory_space=pltpu.SMEM)
BIG = 60 * 1024 * 1024


def split2(value):
    high = value.astype(BF16)
    return high, (value - high.astype(F32)).astype(BF16)


def dot32(left, right, dims=(((1,), (0,)), ((), ()))):
    return lax.dot_general(left, right, dims, preferred_element_type=F32)


def softplus(value):
    return jnp.maximum(value, 0.0) + jnp.log(1.0 + jnp.exp(-jnp.abs(value)))


def sigmoid(value):
    return 1.0 / (1.0 + jnp.exp(-value))


def project_kernel(send_ref, matrix_ref, params_ref, out_ref, rows_ref):
    owned = params_ref.shape[0]
    cameras, _, owners, cap = send_ref.shape
    matrix = matrix_ref[...]
    for block in range(owned):
        rows_ref[block] = jnp.dot(matrix, params_ref[block], precision=HIGHEST, preferred_element_type=F32)
    for owner in range(owners):
        for camera in range(cameras):
            for place in range(cap):
                chosen = send_ref[camera, 0, owner, place]
                first = (camera * cap + place) * PROJ
                out_ref[owner, first : first + PROJ, :] = rows_ref[
                    chosen, camera * 16 : camera * 16 + PROJ, :
                ]


def exchange_kernel(axis, count, x_ref, out_ref, land, send_sems, recv_sems):
    me = lax.axis_index(axis)
    barrier = pltpu.get_barrier_semaphore()
    for step in range(1, count):
        pl.semaphore_signal(
            barrier, inc=1, device_id={axis: lax.rem(me + step, count)}, device_id_type=MESH
        )
    pl.semaphore_wait(barrier, count - 1)
    copies = []
    for step in range(1, count):
        peer = lax.rem(me + step, count)
        copy = pltpu.make_async_remote_copy(
            src_ref=x_ref.at[peer],
            dst_ref=land.at[me],
            send_sem=send_sems.at[step - 1],
            recv_sem=recv_sems.at[step - 1],
            device_id={axis: peer},
            device_id_type=MESH,
        )
        copy.start()
        copies.append(copy)
    out_ref[me] = x_ref[me]
    for step in range(1, count):
        copies[step - 1].wait_recv()
        source = lax.rem(me - step + count, count)
        out_ref[source] = land[source]
    for copy in copies:
        copy.wait_send()


def exchange(x, axis, ident):
    count = x.shape[0]
    return pl.pallas_call(
        functools.partial(exchange_kernel, axis, count),
        out_shape=jax.ShapeDtypeStruct(x.shape, F32),
        in_specs=[VMEM],
        out_specs=VMEM,
        scratch_shapes=[
            pltpu.VMEM(x.shape, F32),
            pltpu.SemaphoreType.DMA((count - 1,)),
            pltpu.SemaphoreType.DMA((count - 1,)),
        ],
        compiler_params=pltpu.CompilerParams(
            collective_id=ident, has_side_effects=True, vmem_limit_bytes=BIG
        ),
        name=f"exchange_{ident}",
    )(x)


def return_kernel(owners, groups, x_ref, out_ref, land, zsend, zrecv, csend, crecv):
    me = lax.axis_index("dev")
    group = lax.axis_index("cam")
    barrier = pltpu.get_barrier_semaphore()
    for step in range(1, owners):
        pl.semaphore_signal(
            barrier, inc=1, device_id={"dev": lax.rem(me + step, owners)}, device_id_type=MESH
        )
    for step in range(1, groups):
        pl.semaphore_signal(
            barrier, inc=1, device_id={"cam": lax.rem(group + step, groups)}, device_id_type=MESH
        )
    pl.semaphore_wait(barrier, owners + groups - 2)
    along = []
    for step in range(1, owners):
        peer = lax.rem(me + step, owners)
        copy = pltpu.make_async_remote_copy(
            src_ref=x_ref.at[peer],
            dst_ref=land.at[0, me],
            send_sem=zsend.at[step - 1],
            recv_sem=zrecv.at[step - 1],
            device_id={"dev": peer},
            device_id_type=MESH,
        )
        copy.start()
        along.append(copy)
    across = []
    for step in range(owners):
        source = lax.rem(me - step + owners, owners)
        if step:
            along[step - 1].wait_recv()
        piece = land.at[0, source] if step else x_ref.at[me]
        for turn in range(1, groups):
            copy = pltpu.make_async_remote_copy(
                src_ref=piece,
                dst_ref=land.at[turn, source],
                send_sem=csend.at[turn - 1, step],
                recv_sem=crecv.at[turn - 1, step],
                device_id={"cam": lax.rem(group - turn + groups, groups)},
                device_id_type=MESH,
            )
            copy.start()
            across.append((turn, source, copy))
        out_ref[0, source] = land[0, source] if step else x_ref[me]
    for turn, source, copy in across:
        copy.wait_recv()
        out_ref[turn, source] = land[turn, source]
    for copy in along:
        copy.wait_send()
    for _, _, copy in across:
        copy.wait_send()


def return_home(x, groups):
    owners = x.shape[0]
    shape = (groups,) + x.shape
    return pl.pallas_call(
        functools.partial(return_kernel, owners, groups),
        out_shape=jax.ShapeDtypeStruct(shape, F32),
        in_specs=[VMEM],
        out_specs=VMEM,
        scratch_shapes=[
            pltpu.VMEM(shape, F32),
            pltpu.SemaphoreType.DMA((owners - 1,)),
            pltpu.SemaphoreType.DMA((owners - 1,)),
            pltpu.SemaphoreType.DMA((groups - 1, owners)),
            pltpu.SemaphoreType.DMA((groups - 1, owners)),
        ],
        compiler_params=pltpu.CompilerParams(
            collective_id=7, has_side_effects=True, vmem_limit_bytes=BIG
        ),
        name="return_home",
    )(x)


def shape_of(raw):
    turn_x = jnp.tanh(raw[0])
    turn_y = jnp.tanh(raw[1])
    conic_a = 0.02 + 0.1 * softplus(raw[2])
    conic_c = 0.02 + 0.1 * softplus(raw[4])
    turn_b = jnp.tanh(raw[3])
    root = jnp.sqrt(conic_a * conic_c)
    return turn_x, turn_y, conic_a, conic_c, turn_b, root


def render_kernel(
    slot_ref, count_ref, received_ref, target_ref, image_ref, back_ref,
    feats, grads, weights, pairs, ratios, carry, before, after_tri, cot_rows, cot_cols, picture,
):
    cameras, tiles, _ = slot_ref.shape
    owners, rows, splats = received_ref.shape
    cap = rows // (PROJ * cameras)
    centre = 0.5 * TSIDE
    spread = 0.375 * TSIDE
    pixels = TSIDE * TSIDE
    half = 128
    per_chunk = half // TSIDE

    feats[...] = jnp.zeros(feats.shape, F32)
    grads[...] = jnp.zeros(grads.shape, F32)
    for index in range(cameras * cap):
        raw = [received_ref[:, index * PROJ + k, :] for k in range(PROJ)]
        turn_x, turn_y, conic_a, conic_c, turn_b, root = shape_of(raw)
        conic_b = 0.9 * root * turn_b
        feats[:, index, 0, :] = centre + spread * turn_x
        feats[:, index, 1, :] = centre + spread * turn_y
        feats[:, index, 2, :] = (0.5 * LOG2E) * conic_a
        feats[:, index, 3, :] = LOG2E * conic_b
        feats[:, index, 4, :] = (0.5 * LOG2E) * conic_c
        feats[:, index, 5, :] = math.log2(0.99) - LOG2E * softplus(6.0 - raw[5])
        for k in range(3):
            feats[:, index, 8 + k, :] = sigmoid(raw[6 + k])

    row = lax.broadcasted_iota(jnp.int32, (splats, splats), 0)
    column = lax.broadcasted_iota(jnp.int32, (splats, splats), 1)
    ones = jnp.ones((splats, splats), BF16)
    lower = jnp.where(row < column, 1.0, 0.0).astype(BF16)
    upper = jnp.where(row > column, 1.0, 0.0).astype(BF16)
    for part in range(2):
        before[part * splats : (part + 1) * splats, :splats] = lower
        before[part * splats : (part + 1) * splats, splats:] = ones
        after_tri[part * splats : (part + 1) * splats, :splats] = upper
        after_tri[part * splats : (part + 1) * splats, splats:] = ones
    grid = lax.broadcasted_iota(jnp.int32, (TSIDE, splats), 0).astype(F32) + 0.5
    pad_rows = jnp.zeros((8, splats), F32)

    def entry_of(camera, tile, position):
        slot = slot_ref[camera, tile, position]
        return slot // cap, camera * cap + slot % cap

    def tile_step(number, _):
        camera = number // tiles
        tile = number % tiles
        live = count_ref[camera, tile]
        carry[...] = jnp.zeros(carry.shape, F32)
        picture[...] = jnp.zeros(picture.shape, F32)

        def forward(position, _):
            owner, index = entry_of(camera, tile, position)
            part = lambda k: feats[owner, index, k : k + 1, :]
            off_x = grid - part(0)
            off_y = grid - part(1)
            in_x = -(part(2) * off_x * off_x)
            cross = -(part(3) * off_x)
            in_y = part(5) - part(4) * off_y * off_y
            for chunk in range(pixels // half):
                where = slice(chunk * half, (chunk + 1) * half)
                lines = []
                for line in range(chunk * per_chunk, (chunk + 1) * per_chunk):
                    lines.append(in_x + (in_y[line : line + 1] + cross * off_y[line : line + 1]))
                alpha = jnp.exp2(jnp.concatenate(lines, axis=0))
                log_keep = jnp.log2(1.0 - alpha)
                summed = dot32(jnp.concatenate(split2(log_keep), axis=1), before[...])
                held = carry[where, :]
                weight = alpha * jnp.exp2(summed[:, :splats] + held)
                carry[where, :] = held + summed[:, splats:]
                weights[position, where, :] = weight
                pairs[position, where, :] = jnp.concatenate(split2(weight), axis=1)
                ratios[position, where, :] = alpha * jnp.exp2(-log_keep)
            colour_high, colour_low = split2(feats[owner, index, 8:16, :])
            colour_high = colour_high.astype(F32)
            colour_low = colour_low.astype(F32)
            shades = jnp.concatenate(
                [
                    jnp.concatenate([colour_high, colour_low], axis=0),
                    jnp.concatenate([colour_high, pad_rows], axis=0),
                ],
                axis=1,
            ).astype(BF16)
            drawn = dot32(shades, pairs[position], (((1,), (1,)), ((), ())))
            picture[...] += drawn[:8] + drawn[8:]
            return 0

        lax.fori_loop(0, live, forward, 0)
        colour = picture[0:3, :]
        image_ref[camera, tile] = colour
        picture[0:3, :] = LOSS_WEIGHT * (colour - target_ref[camera, tile])
        cot_high, cot_low = split2(picture[...])
        cot_high = cot_high.astype(F32)
        cot_low = cot_low.astype(F32)
        cot_rows[...] = jnp.concatenate([cot_high, cot_low], axis=0).astype(BF16)
        stacked = jnp.concatenate(
            [cot_high, cot_low, cot_high, jnp.zeros((half - 24, pixels), F32)], axis=0
        )
        cot_cols[...] = stacked.T.astype(BF16)
        carry[...] = jnp.zeros(carry.shape, F32)

        def backward(reverse, _):
            position = live - 1 - reverse
            owner, index = entry_of(camera, tile, position)
            part = lambda k: feats[owner, index, k : k + 1, :]
            off_x = grid - part(0)
            off_y = grid - part(1)
            colour_high, colour_low = split2(feats[owner, index, 8:16, :])
            colour_high = colour_high.astype(F32)
            shades = jnp.concatenate(
                [colour_high, colour_high, colour_low.astype(F32), jnp.zeros((half - 24, splats), F32)],
                axis=0,
            ).astype(BF16)
            total0 = jnp.zeros((TSIDE, splats), F32)
            total1 = jnp.zeros((TSIDE, splats), F32)
            total2 = jnp.zeros((TSIDE, splats), F32)
            for chunk in range(pixels // half):
                where = slice(chunk * half, (chunk + 1) * half)
                shade = dot32(cot_cols[where, :], shades)
                shaded = shade * weights[position, where, :]
                summed = dot32(jnp.concatenate(split2(shaded), axis=1), after_tri[...])
                held = carry[where, :]
                carry[where, :] = held + summed[:, splats:]
                pull = shaded - (summed[:, :splats] + held) * ratios[position, where, :]
                for line in range(per_chunk):
                    height = off_y[chunk * per_chunk + line : chunk * per_chunk + line + 1]
                    piece = pull[line * TSIDE : (line + 1) * TSIDE]
                    lifted = piece * height
                    total0 += piece
                    total1 += lifted
                    total2 += lifted * height
            sum_of = lambda value: jnp.sum(value, axis=0, keepdims=True)
            wide = total0 * off_x
            moments = jnp.concatenate(
                [
                    sum_of(total0),
                    sum_of(wide),
                    sum_of(total1),
                    sum_of(wide * off_x),
                    sum_of(total1 * off_x),
                    sum_of(total2),
                    jnp.zeros((2, splats), F32),
                ],
                axis=0,
            )
            tinted = dot32(cot_rows[...], pairs[position])
            grads[owner, index, 0:8, :] += moments
            grads[owner, index, 8:16, :] += (
                tinted[:8, :splats] + tinted[8:, :splats] + tinted[:8, splats:]
            )
            return 0

        lax.fori_loop(0, live, backward, 0)
        return 0

    lax.fori_loop(0, cameras * tiles, tile_step, 0)

    for index in range(cameras * cap):
        raw = [received_ref[:, index * PROJ + k, :] for k in range(PROJ)]
        turn_x, turn_y, conic_a, conic_c, turn_b, root = shape_of(raw)
        conic_b = 0.9 * root * turn_b
        sum0, sum_x, sum_y, sum_xx, sum_xy, sum_yy = [grads[:, index, k, :] for k in range(6)]
        grad_b = -sum_xy
        grad_a = -0.5 * sum_xx + grad_b * (0.5 * conic_b / conic_a)
        grad_c = -0.5 * sum_yy + grad_b * (0.5 * conic_b / conic_c)
        results = [
            (conic_a * sum_x + conic_b * sum_y) * (spread * (1.0 - turn_x * turn_x)),
            (conic_b * sum_x + conic_c * sum_y) * (spread * (1.0 - turn_y * turn_y)),
            grad_a * (0.1 * sigmoid(raw[2])),
            grad_b * (0.9 * root * (1.0 - turn_b * turn_b)),
            grad_c * (0.1 * sigmoid(raw[4])),
            sum0 * sigmoid(6.0 - raw[5]),
        ]
        for k in range(3):
            tone = sigmoid(raw[6 + k])
            results.append(grads[:, index, 8 + k, :] * (tone * (1.0 - tone)))
        for k in range(PROJ):
            back_ref[:, index * PROJ + k, :] = results[k]


def render(slots, counts, received, targets):
    owners, rows, splats = received.shape
    cameras, tiles, depth = slots.shape
    pixels = targets.shape[-1]
    cap = rows // (PROJ * cameras)
    return pl.pallas_call(
        render_kernel,
        out_shape=(
            jax.ShapeDtypeStruct(targets.shape, F32),
            jax.ShapeDtypeStruct(received.shape, F32),
        ),
        in_specs=[SMEM, SMEM, VMEM, VMEM],
        out_specs=(VMEM, VMEM),
        scratch_shapes=[
            pltpu.VMEM((owners, cameras * cap, 16, splats), F32),
            pltpu.VMEM((owners, cameras * cap, 16, splats), F32),
            pltpu.VMEM((depth, pixels, splats), F32),
            pltpu.VMEM((depth, pixels, 2 * splats), BF16),
            pltpu.VMEM((depth, pixels, splats), F32),
            pltpu.VMEM((pixels, splats), F32),
            pltpu.VMEM((2 * splats, 2 * splats), BF16),
            pltpu.VMEM((2 * splats, 2 * splats), BF16),
            pltpu.VMEM((16, pixels), BF16),
            pltpu.VMEM((pixels, 128), BF16),
            pltpu.VMEM((8, pixels), F32),
        ],
        compiler_params=pltpu.CompilerParams(vmem_limit_bytes=BIG),
        cost_estimate=pl.CostEstimate(
            flops=20_000_000_000, bytes_accessed=100_000_000, transcendentals=4_000_000
        ),
        name="render",
    )(slots, counts, received, targets)


def update_kernel(groups, *refs):
    send_ref, split_ref, live_ref, back_ref, matrix_ref, params_ref = refs[:6]
    firsts = refs[6 : 6 + groups]
    seconds = refs[6 + groups : 6 + 2 * groups]
    params_out, first_out, second_out, parent_out, table = refs[6 + 2 * groups :]
    me = lax.axis_index("cam")
    cameras, owners, cap = send_ref.shape[1:]
    share = firsts[0].shape[0]
    values = params_ref.shape[1]
    splats = params_ref.shape[2]
    table[...] = jnp.zeros(table.shape, F32)
    for turn in range(groups):
        for owner in range(owners):
            for camera in range(cameras):
                for place in range(cap):
                    block = send_ref[turn, camera, owner, place]
                    first = (camera * cap + place) * PROJ
                    into = (turn * cameras + camera) * 16
                    table[block, into : into + PROJ, :] += back_ref[
                        turn, owner, first : first + PROJ, :
                    ]
    matrix_high, matrix_low = split2(matrix_ref[...])
    both = jnp.concatenate([matrix_high, matrix_low], axis=1)
    for turn in range(groups):
        base = lax.rem(me + turn, groups) * share

        def block_step(place, _, turn=turn, base=base):
            block = base + place
            high, low = split2(table[block])
            gradient = dot32(both, jnp.concatenate([high, high], axis=0)) + dot32(matrix_high, low)
            gradient = gradient[:values]
            new_first = BETA_FIRST * firsts[turn][place] + (1.0 - BETA_FIRST) * gradient
            new_second = (
                BETA_SECOND * seconds[turn][place] + (1.0 - BETA_SECOND) * gradient * gradient
            )
            params_out[block] = params_ref[block] - RATE * new_first / (
                jnp.sqrt(new_second) + EPSILON
            )
            if turn == 0:
                first_out[place] = new_first
                second_out[place] = new_second
            return 0

        lax.fori_loop(0, share, block_step, 0, unroll=2)
    for owner in range(split_ref.shape[1]):
        alive = live_ref[0, owner].astype(F32)
        parent_out[owner, 0:values, :] = params_out[split_ref[0, owner]] * alive
        parent_out[owner, values : values + 1, :] = jnp.zeros((1, splats), F32) + alive


def update(send, split_block, split_live, back, matrix, params, firsts, seconds):
    groups = len(firsts)
    owned, values, splats = params.shape
    share = firsts[0].shape
    return pl.pallas_call(
        functools.partial(update_kernel, groups),
        out_shape=(
            jax.ShapeDtypeStruct(params.shape, F32),
            jax.ShapeDtypeStruct(share, F32),
            jax.ShapeDtypeStruct(share, F32),
            jax.ShapeDtypeStruct((split_block.shape[1], values + 1, splats), F32),
        ),
        in_specs=[SMEM, SMEM, SMEM] + [VMEM] * (3 + 2 * groups),
        out_specs=(VMEM,) * 4,
        scratch_shapes=[pltpu.VMEM((owned, matrix.shape[1], splats), F32)],
        compiler_params=pltpu.CompilerParams(vmem_limit_bytes=BIG),
        name="update",
    )(send, split_block, split_live, back, matrix, params, *firsts, *seconds)


def body(
    params, moment_first, moment_second, cam_proj, send_block,
    tile_slot, tile_count, targets, split_block, split_live,
):
    groups = lax.axis_size("cam")
    owners = lax.axis_size("dev")
    cameras, rows, values = cam_proj.shape
    cap = send_block.shape[3]
    splats = params.shape[2]
    padded = jnp.pad(cam_proj, ((0, 0), (0, 16 - rows), (0, 0)))
    outgoing = pl.pallas_call(
        project_kernel,
        out_shape=jax.ShapeDtypeStruct((owners, cameras * cap * PROJ, splats), F32),
        in_specs=[SMEM, VMEM, VMEM],
        out_specs=VMEM,
        scratch_shapes=[pltpu.VMEM((params.shape[0], cameras * 16, splats), F32)],
        compiler_params=pltpu.CompilerParams(vmem_limit_bytes=BIG),
        name="project",
    )(send_block, padded.reshape(cameras * 16, values), params)

    small = jnp.concatenate([padded.reshape(-1), send_block.astype(F32).reshape(-1)])
    smalls = [small]
    firsts = [moment_first[0, 0]]
    seconds = [moment_second[0, 0]]
    for turn in range(1, groups):
        pattern = [((one + turn) % groups, one) for one in range(groups)]
        smalls.append(lax.ppermute(small, "cam", pattern))
        firsts.append(lax.ppermute(moment_first[0, 0], "cam", pattern))
        seconds.append(lax.ppermute(moment_second[0, 0], "cam", pattern))
    joined = jnp.stack(smalls)
    sized = cameras * 16 * values
    matrix = joined[:, :sized].reshape(groups * cameras * 16, values).T
    matrix = jnp.pad(matrix, ((0, -values % 16), (0, 0)))
    sends = joined[:, sized:].astype(jnp.int32).reshape(groups, cameras, owners, cap)

    received = exchange(outgoing, "dev", 5)
    images, back = render(tile_slot, tile_count, received, targets)
    gathered = return_home(back, groups)
    new_params, new_first, new_second, parents = update(
        sends, split_block, split_live, gathered, matrix, params, firsts, seconds
    )
    arrived = exchange(parents, "dev", 6)
    alive = arrived[:, values:, :]
    parent = arrived[:, :values, :]
    offset = 0.5 * jnp.exp(parent[:, 3:6] - 1.0) * alive
    offset = jnp.pad(offset, ((0, 0), (0, values - 3), (0, 0)))
    line = lax.broadcasted_iota(jnp.int32, parent.shape, 1)
    shrunk = parent - jnp.where((line >= 3) & (line < 6), SHRINK, 0.0) * alive
    children = jnp.stack([shrunk + offset, shrunk - offset], axis=1)
    return (
        images,
        new_params,
        new_first.reshape(moment_first.shape),
        new_second.reshape(moment_second.shape),
        children,
    )


def solution(mesh):
    placed = (
        P("dev", None, None),
        P("dev", "cam", None, None, None),
        P("dev", "cam", None, None, None),
        P("cam", None, None),
        P("cam", "dev", None, None),
        P("cam", "dev", None),
        P("cam", "dev"),
        P("cam", "dev", None, None),
        P("dev", None),
        P("dev", None),
    )
    return jax.shard_map(
        body,
        mesh=mesh,
        in_specs=placed,
        out_specs=(
            P("cam", "dev", None, None),
            P("dev", None, None),
            P("dev", "cam", None, None, None),
            P("dev", "cam", None, None, None),
            P("dev", None, None, None),
        ),
        check_vma=False,
    )
```

time: 276 us -> 112 us (0.41); the launches traced: 274 us -> 113 us
  Pallas kernels: 0 us -> 70.3 us
  blocking collectives: 67.8 us -> 0 us
  waiting for transfers between devices: 65.1 us -> 14.1 us
  matrix products: 50.8 us -> 0 us
  loops' own time: 19.2 us -> 0 us
  other arithmetic: 17.4 us -> 2.08 us
  between operations: 14.6 us -> 0.91 us
  local copies, waits for them, and re-layouts: 26 us -> 16.8 us
  starting transfers between devices: 13.4 us -> 8.82 us
    pallas_call x0 -> x6, Pallas kernels: none -> 70.3 us  [the longest x2 22.1 us: exchange(): pl.pallas_call(functools.partial(exchange_kernel, axis, count), out_shape...]
    dot_general x72 -> x0, matrix products: 50.8 us -> none  [the longest x22 14.7 us: advance(): log_before = jnp.einsum('st,dtp->dsp', strict, log_keep, precision=PRECISE)]
    psum x1 -> x0, waiting for transfers between devices: 49.4 us -> none  [body(): summed_grad = lax.psum(gradient, 'cam')]
    all_to_all x1 -> x0, blocking collectives: 49 us -> none  [body(): lax.all_to_all(jnp.stack(buffers), 'dev', split_axis=1, concat_axis=1, ti...]
    another operation x4 -> x0, loops' own time: 19.2 us -> none  [the longest x2 9.95 us: render_grad(): return lax.fori_loop(0, jnp.max(counts), advance, start_state)[2]]
    all_gather x1 -> x0, blocking collectives: 18.8 us -> none  [body(): new_params = lax.all_gather(new_share, 'cam', axis=0, tiled=True)]
    all_to_all x2 -> x0, waiting for transfers between devices: 15.7 us -> none  [the longest x1 11.2 us: body(): lax.all_to_all(outgoing_children, 'dev', split_axis=0, concat_axis=0, til...]
    ppermute x0 -> x9, waiting for transfers between devices: none -> 14.1 us  [the longest x3 11.2 us: body(): seconds.append(lax.ppermute(moment_second[0, 0], 'cam', pattern))]
  transfers between devices with their start and end apart: 3 -> 9, of which waited for: 3 -> 4; matrix products, arithmetic and copies ran while one was open for 1% -> 7% of each run, Pallas kernels for 0% -> 46%
where the time goes in v1:
time: 112 us; the launch traced here: 113 us
  Pallas kernels  70.3 us (63%)
  local copies, waits for them, and re-layouts  16.8 us (15%)
  waiting for transfers between devices  14.1 us (13%)
  starting transfers between devices  8.82 us (8%)
  other arithmetic  2.08 us (2%)
    pallas_call x2, Pallas kernels, exchange(): pl.pallas_call(functools.partial(exchange_kernel, axis, count), out_shape...  22.1 us
    pallas_call x1, Pallas kernels, return_home(): pl.pallas_call(functools.partial(return_kernel, owners, groups), out_shap...  21 us
    pallas_call x1, Pallas kernels, render(): pl.pallas_call(render_kernel, out_shape=(jax.ShapeDtypeStruct(targets.sha...  17.4 us
    unnamed x41, local copies, waits for them, and re-layouts  14 us
    ppermute x3, waiting for transfers between devices, body(): seconds.append(lax.ppermute(moment_second[0, 0], 'cam', pattern))  11.2 us
    pallas_call x1, Pallas kernels, update(): pl.pallas_call(functools.partial(update_kernel, groups), out_shape=(jax.S...  6.9 us
    ppermute x3, starting transfers between devices, body(): smalls.append(lax.ppermute(small, 'cam', pattern))  4.42 us
    pallas_call x1, Pallas kernels, body(): pl.pallas_call(project_kernel, out_shape=jax.ShapeDtypeStruct((owners, ca...  2.87 us
  transfers between devices with their start and end apart: 9, of which 4 were waited for; matrix products, arithmetic and copies ran while one was open for 7% of the time, Pallas kernels for 46%

profile of v1, /device:TPU:1, one launch (start us, length us, event | category | flops | bytes accessed | tf_op | source)
XLA Modules:
  0.0 113.0 jit_solution(6834917024403756811)
XLA Ops:
  0.6 0.7 copy.46
  1.4 0.1 copy.34
  1.4 0.1 reshape.33
  1.5 0.0 copy-start.11
  1.6 0.1 reshape.32
  1.7 0.1 pad_maximum_fusion.4
  1.7 0.4 copy-done.11
  2.2 2.0 %collective-permute-start.2 = (f32[1920]{0:T(1024)S(1)}, f32[1920]{0:T(1024)S(1)}, u32[]{:S(2)}, u32[]{:S(2)}) collective-permute-start(f32[1920]{0:T(1024)S(1)} %pad_maximum_fusion.4), channel_id=1, source_target_pairs={{24,0},{0,8},{8,16},{16,24},{25,1},{1,9},{9,17},{17,25},{26,2},{2,... | collective-permute-start | bytes 23048 | tf_op jit(solution)/shard_map/ppermute | solution.py:507
  4.2 1.2 %collective-permute-start.1 = (f32[1920]{0:T(1024)S(1)}, f32[1920]{0:T(1024)S(1)}, u32[]{:S(2)}, u32[]{:S(2)}) collective-permute-start(f32[1920]{0:T(1024)S(1)} %pad_maximum_fusion.4), channel_id=1, source_target_pairs={{16,0},{24,8},{0,16},{8,24},{17,1},{25,9},{1,17},{9,25},{18,2},{26... | collective-permute-start | bytes 23048 | tf_op jit(solution)/shard_map/ppermute | solution.py:507
  5.4 1.2 %collective-permute-start = (f32[1920]{0:T(1024)S(1)}, f32[1920]{0:T(1024)S(1)}, u32[]{:S(2)}, u32[]{:S(2)}) collective-permute-start(f32[1920]{0:T(1024)S(1)} %pad_maximum_fusion.4), channel_id=1, source_target_pairs={{8,0},{16,8},{24,16},{0,24},{9,1},{17,9},{25,17},{1,25},{10,2},{18... | collective-permute-start | bytes 23048 | tf_op jit(solution)/shard_map/ppermute | solution.py:507
  6.6 1.0 copy.50
  7.6 0.0 copy-start
  7.6 0.3 collective-permute-start.3
  7.9 1.2 %collective-permute-start.4 = (f32[8,59,128]{2,1,0:T(8,128)S(1)}, f32[8,59,128]{2,1,0:T(8,128)S(1)}, u32[]{:S(2)}, u32[]{:S(2)}) collective-permute-start(f32[8,59,128]{2,1,0:T(8,128)S(1)} %bitcast.21), channel_id=1, source_target_pairs={{16,0},{24,8},{0,16},{8,24},{17,1},{25,9},{1,17},{9,25},{18,2},{26... | collective-permute-start | bytes 725000 | tf_op jit(solution)/shard_map/ppermute | solution.py:508
  9.1 0.7 copy.30.send_ref
  9.8 2.8 %copy.31.params_ref.refs_5_ = f32[32,59,128]{2,1,0:T(8,128)} copy(f32[32,59,128]{2,0,1:T(8,128)} %param.10) | data formatting | bytes 1933312 | tf_op args[0]
  12.6 2.9 %project.1.x_ref = f32[8,36,128]{2,1,0:T(8,128)} custom-call(s32[2,1,8,2]{3,2,1,0:T(8,128)} %copy.30.send_ref, f32[32,59]{1,0:T(8,128)} %bitcast.30, f32[32,59,128]{2,1,0:T(8,128)} %copy.31.params_ref.refs_5_), custom_call_target="tpu_custom_call" | custom-call | tf_op jit(solution)/shard_map/project/pallas_call | solution.py:491
  15.5 10.5 %exchange_5.1.received_ref = f32[8,36,128]{2,1,0:T(8,128)} custom-call(f32[8,36,128]{2,1,0:T(8,128)} %project.1.x_ref), custom_call_target="tpu_custom_call" | custom-call | tf_op jit(solution)/shard_map/exchange_5/pallas_call | solution.py:94
  26.0 0.6 copy.32.target_ref
  26.6 17.4 %render.1 = (f32[2,2,3,256]{3,2,1,0:T(4,128)}, f32[8,36,128]{2,1,0:T(8,128)}) custom-call(s32[2,2,8]{2,1,0:T(2,128)} %slot_ref.1, s32[2,2]{1,0:T(2,128)} %count_ref.1, f32[8,36,128]{2,1,0:T(8,128)} %exchange_5.1.received_ref, f32[2,2,3,256]{3,2,1,0:T(4,128)} %copy.32.target_ref), custom_call_target="tpu_custom_call" | custom-call | flops 20000000000 | bytes 100000000 | tf_op jit(solution)/shard_map/render/pallas_call | solution.py:382
  44.1 0.7 copy-done.12
  44.8 0.6 copy.41
  45.4 21.0 %return_home.1.refs_3_ = f32[4,8,36,128]{3,2,1,0:T(8,128)} custom-call(f32[8,36,128]{2,1,0:T(8,128)} %get-tuple-element.12.x_ref), custom_call_target="tpu_custom_call" | custom-call | tf_op jit(solution)/shard_map/return_home/pallas_call | solution.py:167
  66.5 0.1 collective-permute-start.5
  66.6 2.4 %collective-permute-start.6 = (f32[8,59,128]{2,1,0:T(8,128)S(1)}, f32[8,59,128]{2,1,0:T(8,128)S(1)}, u32[]{:S(2)}, u32[]{:S(2)}) collective-permute-start(f32[8,59,128]{2,1,0:T(8,128)S(1)} %bitcast.24), channel_id=1, source_target_pairs={{8,0},{16,8},{24,16},{0,24},{9,1},{17,9},{25,17},{1,25},{10,2},{18... | collective-permute-start | bytes 725000 | tf_op jit(solution)/shard_map/ppermute | solution.py:509
  69.0 0.1 collective-permute-start.7
  69.1 0.3 collective-permute-start.8
  69.5 0.1 maximum_convert_fusion
  69.5 0.1 copy.35
  69.6 0.8 copy.39.refs_0_
  70.5 0.1 reshape.35
  70.6 0.1 copy.36
  70.7 0.6 pad.13.refs_4_
  71.3 2.8 %collective-permute-done.5.refs_9_ = f32[8,59,128]{2,1,0:T(8,128)S(1)} collective-permute-done((f32[8,59,128]{2,1,0:T(8,128)S(1)}, f32[8,59,128]{2,1,0:T(8,128)S(1)}, u32[]{:S(2)}, u32[]{:S(2)}) %collective-permute-start.5) | collective-permute-done | bytes 241696 | tf_op jit(solution)/shard_map/ppermute | solution.py:508
  74.2 4.2 %collective-permute-done.6.refs_11_ = f32[8,59,128]{2,1,0:T(8,128)S(1)} collective-permute-done((f32[8,59,128]{2,1,0:T(8,128)S(1)}, f32[8,59,128]{2,1,0:T(8,128)S(1)}, u32[]{:S(2)}, u32[]{:S(2)}) %collective-permute-start.6) | collective-permute-done | bytes 241696 | tf_op jit(solution)/shard_map/ppermute | solution.py:509
  78.4 4.4 %collective-permute-done.7.refs_12_ = f32[8,59,128]{2,1,0:T(8,128)S(1)} collective-permute-done((f32[8,59,128]{2,1,0:T(8,128)S(1)}, f32[8,59,128]{2,1,0:T(8,128)S(1)}, u32[]{:S(2)}, u32[]{:S(2)}) %collective-permute-start.7) | collective-permute-done | bytes 241696 | tf_op jit(solution)/shard_map/ppermute | solution.py:509
  82.8 2.6 %collective-permute-done.8.refs_13_ = f32[8,59,128]{2,1,0:T(8,128)S(1)} collective-permute-done((f32[8,59,128]{2,1,0:T(8,128)S(1)}, f32[8,59,128]{2,1,0:T(8,128)S(1)}, u32[]{:S(2)}, u32[]{:S(2)}) %collective-permute-start.8) | collective-permute-done | bytes 241696 | tf_op jit(solution)/shard_map/ppermute | solution.py:509
  85.4 0.7 copy-done.7
  86.1 6.9 %update.1 = (f32[32,59,128]{2,1,0:T(8,128)}, f32[8,59,128]{2,1,0:T(8,128)}, f32[8,59,128]{2,1,0:T(8,128)}, f32[8,60,128]{2,1,0:T(8,128)}) custom-call(s32[4,2,8,2]{3,2,1,0:T(8,128)} %copy.39.refs_0_, s32[1,8]{1,0:T(1,128)} %refs_1_.1, s32[1,8]{1,0:T(1,128)} %refs_2_.1, f32[4,8,36,128]{3,2,1,0:T(8,128)} %return_home.1.refs_3_, f32[64,128]{1,0:T(8,128)} %pad.13.refs_4_, ...), custom_call_target="tpu_custom_call" | custom-call | tf_op jit(solution)/shard_map/update/pallas_call | solution.py:465
  93.0 2.8 %copy.42 = f32[32,59,128]{2,0,1:T(8,128)} copy(f32[32,59,128]{2,1,0:T(8,128)} %get-tuple-element.23) | data formatting | bytes 1933312
  95.8 0.8 copy.43
  96.6 0.1 copy-done.8
  96.7 0.8 copy.44
  97.6 11.6 %exchange_6.1 = f32[8,60,128]{2,1,0:T(8,128)} custom-call(f32[8,60,128]{2,1,0:T(8,128)} %get-tuple-element.16.x_ref), custom_call_target="tpu_custom_call" | custom-call | tf_op jit(solution)/shard_map/exchange_6/pallas_call | solution.py:94
  109.2 0.8 slice.19
  109.9 0.8 exponential_multiply_fusion
  110.7 1.1 fusion
  111.8 1.2 %copy.45 = f32[8,2,59,128]{3,1,2,0:T(2,128)} copy(f32[8,2,59,128]{3,2,0,1:T(8,128)S(1)} %pad_maximum_fusion) | data formatting | bytes 966656
  (40 shorter events, 0.2 us)
Async XLA Ops:
  0.6 0.7 copy-start.14
  1.5 0.6 copy-start.11
  2.2 64.3 %collective-permute-start.2 = (f32[1920]{0:T(1024)S(1)}, f32[1920]{0:T(1024)S(1)}, u32[]{:S(2)}, u32[]{:S(2)}) collective-permute-start(f32[1920]{0:T(1024)S(1)} %pad_maximum_fusion.4), channel_id=1, source_target_pairs={{24,0},{0,8},{8,16},{16,24},{25,1},{1,9},{9,17},{17,25},{26,2},{2,... | collective-permute-start | bytes 23048 | tf_op jit(solution)/shard_map/ppermute | solution.py:507
  4.2 62.4 %collective-permute-start.1 = (f32[1920]{0:T(1024)S(1)}, f32[1920]{0:T(1024)S(1)}, u32[]{:S(2)}, u32[]{:S(2)}) collective-permute-start(f32[1920]{0:T(1024)S(1)} %pad_maximum_fusion.4), channel_id=1, source_target_pairs={{16,0},{24,8},{0,16},{8,24},{17,1},{25,9},{1,17},{9,25},{18,2},{26... | collective-permute-start | bytes 23048 | tf_op jit(solution)/shard_map/ppermute | solution.py:507
  5.4 63.6 %collective-permute-start = (f32[1920]{0:T(1024)S(1)}, f32[1920]{0:T(1024)S(1)}, u32[]{:S(2)}, u32[]{:S(2)}) collective-permute-start(f32[1920]{0:T(1024)S(1)} %pad_maximum_fusion.4), channel_id=1, source_target_pairs={{8,0},{16,8},{24,16},{0,24},{9,1},{17,9},{25,17},{1,25},{10,2},{18... | collective-permute-start | bytes 23048 | tf_op jit(solution)/shard_map/ppermute | solution.py:507
  7.6 58.9 %copy-start = (f32[1,1,8,59,128]{4,3,2,1,0:T(8,128)}, f32[1,1,8,59,128]{4,3,2,1,0:T(8,128)S(1)}, u32[]{:S(2)}) copy-start(f32[1,1,8,59,128]{4,3,2,1,0:T(8,128)S(1)} %copy.50) | copy-start | bytes 724996
  7.6 61.5 %collective-permute-start.3 = (f32[8,59,128]{2,1,0:T(8,128)S(1)}, f32[8,59,128]{2,1,0:T(8,128)S(1)}, u32[]{:S(2)}, u32[]{:S(2)}) collective-permute-start(f32[8,59,128]{2,1,0:T(8,128)S(1)} %bitcast.20), channel_id=1, source_target_pairs={{8,0},{16,8},{24,16},{0,24},{9,1},{17,9},{25,17},{1,25},{10,2},{18... | collective-permute-start | bytes 725000 | tf_op jit(solution)/shard_map/ppermute | solution.py:508
  7.9 63.4 %collective-permute-start.4 = (f32[8,59,128]{2,1,0:T(8,128)S(1)}, f32[8,59,128]{2,1,0:T(8,128)S(1)}, u32[]{:S(2)}, u32[]{:S(2)}) collective-permute-start(f32[8,59,128]{2,1,0:T(8,128)S(1)} %bitcast.21), channel_id=1, source_target_pairs={{16,0},{24,8},{0,16},{8,24},{17,1},{25,9},{1,17},{9,25},{18,2},{26... | collective-permute-start | bytes 725000 | tf_op jit(solution)/shard_map/ppermute | solution.py:508
  15.5 10.6 %copy-start.13 = (f32[2,2,3,256]{3,1,2,0:T(2,128)S(1)}, f32[2,2,3,256]{3,1,2,0:T(2,128)}, u32[]{:S(2)}) copy-start(f32[2,2,3,256]{3,1,2,0:T(2,128)} %param.17) | copy-start | bytes 36868
  44.1 0.7 copy-start.12
  45.4 21.0 %copy-start.10 = (f32[1,1,8,59,128]{4,2,3,1,0:T(8,128)S(1)}, f32[1,1,8,59,128]{4,2,3,1,0:T(8,128)}, u32[]{:S(2)}) copy-start(f32[1,1,8,59,128]{4,2,3,1,0:T(8,128)} %param.12) | copy-start | bytes 724996
  66.5 18.9 %copy-start.1 = (f32[1,1,8,59,128]{4,3,2,1,0:T(8,128)}, f32[1,1,8,59,128]{4,3,2,1,0:T(8,128)S(1)}, u32[]{:S(2)}) copy-start(f32[1,1,8,59,128]{4,3,2,1,0:T(8,128)S(1)} %copy.49) | copy-start | bytes 724996
  66.5 7.6 %collective-permute-start.5 = (f32[8,59,128]{2,1,0:T(8,128)S(1)}, f32[8,59,128]{2,1,0:T(8,128)S(1)}, u32[]{:S(2)}, u32[]{:S(2)}) collective-permute-start(f32[8,59,128]{2,1,0:T(8,128)S(1)} %bitcast.22), channel_id=1, source_target_pairs={{24,0},{0,8},{8,16},{16,24},{25,1},{1,9},{9,17},{17,25},{26,2},{2,... | collective-permute-start | bytes 725000 | tf_op jit(solution)/shard_map/ppermute | solution.py:508
  66.6 11.8 %collective-permute-start.6 = (f32[8,59,128]{2,1,0:T(8,128)S(1)}, f32[8,59,128]{2,1,0:T(8,128)S(1)}, u32[]{:S(2)}, u32[]{:S(2)}) collective-permute-start(f32[8,59,128]{2,1,0:T(8,128)S(1)} %bitcast.24), channel_id=1, source_target_pairs={{8,0},{16,8},{24,16},{0,24},{9,1},{17,9},{25,17},{1,25},{10,2},{18... | collective-permute-start | bytes 725000 | tf_op jit(solution)/shard_map/ppermute | solution.py:509
  69.0 13.8 %collective-permute-start.7 = (f32[8,59,128]{2,1,0:T(8,128)S(1)}, f32[8,59,128]{2,1,0:T(8,128)S(1)}, u32[]{:S(2)}, u32[]{:S(2)}) collective-permute-start(f32[8,59,128]{2,1,0:T(8,128)S(1)} %bitcast.25), channel_id=1, source_target_pairs={{16,0},{24,8},{0,16},{8,24},{17,1},{25,9},{1,17},{9,25},{18,2},{26... | collective-permute-start | bytes 725000 | tf_op jit(solution)/shard_map/ppermute | solution.py:509
  69.1 16.3 %copy-start.2 = (f32[8,59,128]{2,1,0:T(8,128)}, f32[8,59,128]{2,1,0:T(8,128)S(1)}, u32[]{:S(2)}) copy-start(f32[8,59,128]{2,1,0:T(8,128)S(1)} %collective-permute-done.3.refs_7_) | copy-start | bytes 724996
  69.1 16.3 %collective-permute-start.8 = (f32[8,59,128]{2,1,0:T(8,128)S(1)}, f32[8,59,128]{2,1,0:T(8,128)S(1)}, u32[]{:S(2)}, u32[]{:S(2)}) collective-permute-start(f32[8,59,128]{2,1,0:T(8,128)S(1)} %bitcast.26), channel_id=1, source_target_pairs={{24,0},{0,8},{8,16},{16,24},{25,1},{1,9},{9,17},{17,25},{26,2},{2,... | collective-permute-start | bytes 725000 | tf_op jit(solution)/shard_map/ppermute | solution.py:509
  71.3 14.1 %copy-start.3 = (f32[8,59,128]{2,1,0:T(8,128)}, f32[8,59,128]{2,1,0:T(8,128)S(1)}, u32[]{:S(2)}) copy-start(f32[8,59,128]{2,1,0:T(8,128)S(1)} %collective-permute-done.4.refs_8_) | copy-start | bytes 724996
  74.2 11.2 %copy-start.4 = (f32[8,59,128]{2,1,0:T(8,128)}, f32[8,59,128]{2,1,0:T(8,128)S(1)}, u32[]{:S(2)}) copy-start(f32[8,59,128]{2,1,0:T(8,128)S(1)} %collective-permute-done.5.refs_9_) | copy-start | bytes 724996
  78.4 7.0 %copy-start.5 = (f32[8,59,128]{2,1,0:T(8,128)}, f32[8,59,128]{2,1,0:T(8,128)S(1)}, u32[]{:S(2)}) copy-start(f32[8,59,128]{2,1,0:T(8,128)S(1)} %collective-permute-done.6.refs_11_) | copy-start | bytes 724996
  82.8 2.6 %copy-start.6 = (f32[8,59,128]{2,1,0:T(8,128)}, f32[8,59,128]{2,1,0:T(8,128)S(1)}, u32[]{:S(2)}) copy-start(f32[8,59,128]{2,1,0:T(8,128)S(1)} %collective-permute-done.7.refs_12_) | copy-start | bytes 724996
  85.4 0.7 copy-start.7
  93.0 2.8 %copy-start.9 = (f32[8,59,128]{2,1,0:T(8,128)S(1)}, f32[8,59,128]{2,1,0:T(8,128)}, u32[]{:S(2)}) copy-start(f32[8,59,128]{2,1,0:T(8,128)} %get-tuple-element.14) | copy-start | bytes 724996
  95.8 0.9 copy-start.8

commit v2 on v1

--- a/solution.py
+++ b/solution.py
@@ -43,20 +43,74 @@
     return 1.0 / (1.0 + jnp.exp(-value))
 
 
-def project_kernel(send_ref, matrix_ref, params_ref, out_ref, rows_ref):
-    owned = params_ref.shape[0]
+def project_kernel(
+    send_ref, matrix_ref, params_ref, out_ref, rows_ref, parcels, land, send_sems, recv_sems
+):
+    values, owned, _ = params_ref.shape
     cameras, _, owners, cap = send_ref.shape
-    matrix = matrix_ref[...]
+    me = lax.axis_index("dev")
+    barrier = pltpu.get_barrier_semaphore()
+    for step in range(1, owners):
+        pl.semaphore_signal(
+            barrier, inc=1, device_id={"dev": lax.rem(me + step, owners)}, device_id_type=MESH
+        )
+    matrix = matrix_ref[:, :values]
     for block in range(owned):
-        rows_ref[block] = jnp.dot(matrix, params_ref[block], precision=HIGHEST, preferred_element_type=F32)
+        rows_ref[block] = jnp.dot(
+            matrix, params_ref[:, block, :], precision=HIGHEST, preferred_element_type=F32
+        )
     for owner in range(owners):
         for camera in range(cameras):
             for place in range(cap):
                 chosen = send_ref[camera, 0, owner, place]
                 first = (camera * cap + place) * PROJ
-                out_ref[owner, first : first + PROJ, :] = rows_ref[
+                parcels[owner, first : first + PROJ, :] = rows_ref[
                     chosen, camera * 16 : camera * 16 + PROJ, :
                 ]
+    pl.semaphore_wait(barrier, owners - 1)
+    copies = []
+    for step in range(1, owners):
+        peer = lax.rem(me + step, owners)
+        copy = pltpu.make_async_remote_copy(
+            src_ref=parcels.at[peer],
+            dst_ref=land.at[me],
+            send_sem=send_sems.at[step - 1],
+            recv_sem=recv_sems.at[step - 1],
+            device_id={"dev": peer},
+            device_id_type=MESH,
+        )
+        copy.start()
+        copies.append(copy)
+    out_ref[me] = parcels[me]
+    for step in range(1, owners):
+        copies[step - 1].wait_recv()
+        source = lax.rem(me - step + owners, owners)
+        out_ref[source] = land[source]
+    for copy in copies:
+        copy.wait_send()
+
+
+def project(send_block, matrix, params):
+    cameras, _, owners, cap = send_block.shape
+    values, owned, splats = params.shape
+    shape = (owners, cameras * cap * PROJ, splats)
+    return pl.pallas_call(
+        project_kernel,
+        out_shape=jax.ShapeDtypeStruct(shape, F32),
+        in_specs=[SMEM, VMEM, VMEM],
+        out_specs=VMEM,
+        scratch_shapes=[
+            pltpu.VMEM((owned, matrix.shape[0], splats), F32),
+            pltpu.VMEM(shape, F32),
+            pltpu.VMEM(shape, F32),
+            pltpu.SemaphoreType.DMA((owners - 1,)),
+            pltpu.SemaphoreType.DMA((owners - 1,)),
+        ],
+        compiler_params=pltpu.CompilerParams(
+            collective_id=5, has_side_effects=True, vmem_limit_bytes=BIG
+        ),
+        name="project",
+    )(send_block, matrix, params)
 
 
 def exchange_kernel(axis, count, x_ref, out_ref, land, send_sems, recv_sems):
@@ -282,9 +336,12 @@
             return 0
 
         lax.fori_loop(0, live, forward, 0)
-        colour = picture[0:3, :]
-        image_ref[camera, tile] = colour
-        picture[0:3, :] = LOSS_WEIGHT * (colour - target_ref[camera, tile])
+        for k in range(3):
+            colour = picture[k : k + 1, :]
+            image_ref[camera, k, pl.ds(tile, 1), :] = colour
+            picture[k : k + 1, :] = LOSS_WEIGHT * (
+                colour - target_ref[camera, k, pl.ds(tile, 1), :]
+            )
         cot_high, cot_low = split2(picture[...])
         cot_high = cot_high.astype(F32)
         cot_low = cot_low.astype(F32)
@@ -409,73 +466,110 @@
 
 
 def update_kernel(groups, *refs):
-    send_ref, split_ref, live_ref, back_ref, matrix_ref, params_ref = refs[:6]
-    firsts = refs[6 : 6 + groups]
-    seconds = refs[6 + groups : 6 + 2 * groups]
-    params_out, first_out, second_out, parent_out, table = refs[6 + 2 * groups :]
+    send_ref, split_ref, live_ref, back_ref, params_ref = refs[:5]
+    packs = refs[5 : 5 + groups]
+    params_out, first_out, second_out, parent_out, table, slopes = refs[5 + groups :]
     me = lax.axis_index("cam")
-    cameras, owners, cap = send_ref.shape[1:]
-    share = firsts[0].shape[0]
-    values = params_ref.shape[1]
-    splats = params_ref.shape[2]
+    owners, rows = back_ref.shape[1:3]
+    values, share, splats = first_out.shape
+    cameras = table.shape[1] // (16 * groups)
+    cap = rows // (PROJ * cameras)
     table[...] = jnp.zeros(table.shape, F32)
     for turn in range(groups):
         for owner in range(owners):
             for camera in range(cameras):
                 for place in range(cap):
-                    block = send_ref[turn, camera, owner, place]
+                    block = send_ref[turn, (camera * owners + owner) * cap + place]
                     first = (camera * cap + place) * PROJ
                     into = (turn * cameras + camera) * 16
                     table[block, into : into + PROJ, :] += back_ref[
                         turn, owner, first : first + PROJ, :
                     ]
-    matrix_high, matrix_low = split2(matrix_ref[...])
+    held = values * share
+    stacked = jnp.concatenate(
+        [pack[2 * held : 2 * held + 16 * cameras, :] for pack in packs], axis=0
+    )
+    matrix_high, matrix_low = split2(stacked.T[: -(-values // 16) * 16])
     both = jnp.concatenate([matrix_high, matrix_low], axis=1)
     for turn in range(groups):
-        base = lax.rem(me + turn, groups) * share
-
-        def block_step(place, _, turn=turn, base=base):
-            block = base + place
-            high, low = split2(table[block])
+        base = pl.multiple_of(lax.rem(me + turn, groups) * share, share)
+        for place in range(share):
+            high, low = split2(table[base + place])
             gradient = dot32(both, jnp.concatenate([high, high], axis=0)) + dot32(matrix_high, low)
-            gradient = gradient[:values]
-            new_first = BETA_FIRST * firsts[turn][place] + (1.0 - BETA_FIRST) * gradient
-            new_second = (
-                BETA_SECOND * seconds[turn][place] + (1.0 - BETA_SECOND) * gradient * gradient
-            )
-            params_out[block] = params_ref[block] - RATE * new_first / (
-                jnp.sqrt(new_second) + EPSILON
-            )
+            slopes[:, place, :] = gradient[:values]
+        pack = packs[turn]
+        for start in range(0, values, 8):
+            end = min(values, start + 8)
+            size = (end - start, share, splats)
+            gradient = slopes[start:end]
+            first = pack[start * share : end * share, :].reshape(size)
+            second = pack[held + start * share : held + end * share, :].reshape(size)
+            new_first = BETA_FIRST * first + (1.0 - BETA_FIRST) * gradient
+            new_second = BETA_SECOND * second + (1.0 - BETA_SECOND) * gradient * gradient
+            params_out[start:end, pl.ds(base, share), :] = params_ref[
+                start:end, pl.ds(base, share), :
+            ] - RATE * new_first / (jnp.sqrt(new_second) + EPSILON)
             if turn == 0:
-                first_out[place] = new_first
-                second_out[place] = new_second
-            return 0
-
-        lax.fori_loop(0, share, block_step, 0, unroll=2)
+                first_out[start:end] = new_first
+                second_out[start:end] = new_second
     for owner in range(split_ref.shape[1]):
         alive = live_ref[0, owner].astype(F32)
-        parent_out[owner, 0:values, :] = params_out[split_ref[0, owner]] * alive
+        chosen = params_out[:, pl.ds(split_ref[0, owner], 1), :].reshape(values, splats)
+        parent_out[owner, 0:values, :] = chosen * alive
         parent_out[owner, values : values + 1, :] = jnp.zeros((1, splats), F32) + alive
 
 
-def update(send, split_block, split_live, back, matrix, params, firsts, seconds):
-    groups = len(firsts)
-    owned, values, splats = params.shape
-    share = firsts[0].shape
+def update(sends, split_block, split_live, back, params, packs, share, cameras):
+    groups = len(packs)
+    values, owned, splats = params.shape
+    moments = jax.ShapeDtypeStruct((values, share, splats), F32)
     return pl.pallas_call(
         functools.partial(update_kernel, groups),
         out_shape=(
             jax.ShapeDtypeStruct(params.shape, F32),
-            jax.ShapeDtypeStruct(share, F32),
-            jax.ShapeDtypeStruct(share, F32),
+            moments,
+            moments,
             jax.ShapeDtypeStruct((split_block.shape[1], values + 1, splats), F32),
         ),
-        in_specs=[SMEM, SMEM, SMEM] + [VMEM] * (3 + 2 * groups),
+        in_specs=[SMEM, SMEM, SMEM] + [VMEM] * (2 + groups),
         out_specs=(VMEM,) * 4,
-        scratch_shapes=[pltpu.VMEM((owned, matrix.shape[1], splats), F32)],
+        scratch_shapes=[
+            pltpu.VMEM((owned, groups * 16 * cameras, splats), F32),
+            pltpu.VMEM((values, share, splats), F32),
+        ],
         compiler_params=pltpu.CompilerParams(vmem_limit_bytes=BIG),
         name="update",
-    )(send, split_block, split_live, back, matrix, params, *firsts, *seconds)
+    )(sends, split_block, split_live, back, params, *packs)
+
+
+def divide_kernel(parent_ref, child_ref):
+    values = parent_ref.shape[1] - 1
+    line = lax.broadcasted_iota(jnp.int32, (values, parent_ref.shape[2]), 0)
+    for owner in range(parent_ref.shape[0]):
+        alive = parent_ref[owner, values : values + 1, :]
+        parent = parent_ref[owner, 0:values, :]
+        shift = jnp.concatenate(
+            [
+                0.5 * jnp.exp(parent[3:6] - 1.0) * alive,
+                jnp.zeros((values - 3, parent.shape[1]), F32),
+            ],
+            axis=0,
+        )
+        shrunk = parent - jnp.where((line >= 3) & (line < 6), SHRINK, 0.0) * alive
+        child_ref[owner, :, 0, :] = shrunk + shift
+        child_ref[owner, :, 1, :] = shrunk - shift
+
+
+def divide(parents):
+    owners, rows, splats = parents.shape
+    return pl.pallas_call(
+        divide_kernel,
+        out_shape=jax.ShapeDtypeStruct((owners, rows - 1, 2, splats), F32),
+        in_specs=[VMEM],
+        out_specs=VMEM,
+        compiler_params=pltpu.CompilerParams(vmem_limit_bytes=BIG),
+        name="divide",
+    )(parents)
 
 
 def body(
@@ -483,56 +577,39 @@
     tile_slot, tile_count, targets, split_block, split_live,
 ):
     groups = lax.axis_size("cam")
-    owners = lax.axis_size("dev")
     cameras, rows, values = cam_proj.shape
-    cap = send_block.shape[3]
-    splats = params.shape[2]
-    padded = jnp.pad(cam_proj, ((0, 0), (0, 16 - rows), (0, 0)))
-    outgoing = pl.pallas_call(
-        project_kernel,
-        out_shape=jax.ShapeDtypeStruct((owners, cameras * cap * PROJ, splats), F32),
-        in_specs=[SMEM, VMEM, VMEM],
-        out_specs=VMEM,
-        scratch_shapes=[pltpu.VMEM((params.shape[0], cameras * 16, splats), F32)],
-        compiler_params=pltpu.CompilerParams(vmem_limit_bytes=BIG),
-        name="project",
-    )(send_block, padded.reshape(cameras * 16, values), params)
-
-    small = jnp.concatenate([padded.reshape(-1), send_block.astype(F32).reshape(-1)])
-    smalls = [small]
-    firsts = [moment_first[0, 0]]
-    seconds = [moment_second[0, 0]]
+    owned, _, splats = params.shape
+    share = moment_first.shape[2]
+    matrix = jnp.pad(cam_proj, ((0, 0), (0, 16 - rows), (0, 128 - values)))
+    matrix = matrix.reshape(cameras * 16, 128)
+    numbers = send_block.astype(F32).reshape(-1)
+    numbers = jnp.pad(numbers, (0, -numbers.size % 1024)).reshape(-1, 128)
+    by_value = lambda moment: moment[0, 0].transpose(1, 0, 2).reshape(values * share, splats)
+    pack = jnp.concatenate([by_value(moment_first), by_value(moment_second), matrix, numbers])
+    packs = [pack]
     for turn in range(1, groups):
         pattern = [((one + turn) % groups, one) for one in range(groups)]
-        smalls.append(lax.ppermute(small, "cam", pattern))
-        firsts.append(lax.ppermute(moment_first[0, 0], "cam", pattern))
-        seconds.append(lax.ppermute(moment_second[0, 0], "cam", pattern))
-    joined = jnp.stack(smalls)
-    sized = cameras * 16 * values
-    matrix = joined[:, :sized].reshape(groups * cameras * 16, values).T
-    matrix = jnp.pad(matrix, ((0, -values % 16), (0, 0)))
-    sends = joined[:, sized:].astype(jnp.int32).reshape(groups, cameras, owners, cap)
-
-    received = exchange(outgoing, "dev", 5)
-    images, back = render(tile_slot, tile_count, received, targets)
+        packs.append(lax.ppermute(pack, "cam", pattern))
+    first_number = 2 * values * share + cameras * 16
+    used = -(-send_block.size // 128)
+    sends = jnp.stack([one[first_number : first_number + used].reshape(-1) for one in packs])
+    sends = sends.astype(jnp.int32)
+
+    by_block = params.transpose(1, 0, 2)
+    received = project(send_block, matrix, by_block)
+    images, back = render(tile_slot, tile_count, received, targets.transpose(0, 2, 1, 3))
     gathered = return_home(back, groups)
     new_params, new_first, new_second, parents = update(
-        sends, split_block, split_live, gathered, matrix, params, firsts, seconds
+        sends, split_block, split_live, gathered, by_block, packs, share, cameras
     )
-    arrived = exchange(parents, "dev", 6)
-    alive = arrived[:, values:, :]
-    parent = arrived[:, :values, :]
-    offset = 0.5 * jnp.exp(parent[:, 3:6] - 1.0) * alive
-    offset = jnp.pad(offset, ((0, 0), (0, values - 3), (0, 0)))
-    line = lax.broadcasted_iota(jnp.int32, parent.shape, 1)
-    shrunk = parent - jnp.where((line >= 3) & (line < 6), SHRINK, 0.0) * alive
-    children = jnp.stack([shrunk + offset, shrunk - offset], axis=1)
+    children = divide(exchange(parents, "dev", 6))
+    restore = lambda moment: moment.transpose(1, 0, 2).reshape(moment_first.shape)
     return (
-        images,
-        new_params,
-        new_first.reshape(moment_first.shape),
-        new_second.reshape(moment_second.shape),
-        children,
+        images.transpose(0, 2, 1, 3),
+        new_params.transpose(1, 0, 2),
+        restore(new_first),
+        restore(new_second),
+        children.transpose(0, 2, 1, 3),
     )
 
 

time: 112 us -> 71.8 us (0.64); the launches traced: 113 us -> 71.1 us
  local copies, waits for them, and re-layouts: 16.8 us -> 1.93 us
  waiting for transfers between devices: 14.1 us -> 0.01 us
  Pallas kernels: 70.3 us -> 61.5 us
  starting transfers between devices: 8.82 us -> 4.47 us
    ppermute x9 -> x3, waiting for transfers between devices: 14.1 us -> 0.01 us  [body(): packs.append(lax.ppermute(pack, 'cam', pattern))]
    unnamed x41 -> x16, local copies, waits for them, and re-layouts: 14 us -> 1.73 us
    pallas_call x2 -> x1, Pallas kernels: 22.1 us -> 10.8 us  [exchange(): pl.pallas_call(functools.partial(exchange_kernel, axis, count), out_shape...]
    pallas_call x1 -> x2, Pallas kernels: 2.87 us -> 12.6 us  [the longest x1 10.6 us: project(): pl.pallas_call(project_kernel, out_shape=jax.ShapeDtypeStruct(shape, F32)...]
    pallas_call x1, Pallas kernels: 21 us -> 15.6 us  [return_home(): pl.pallas_call(functools.partial(return_kernel, owners, groups), out_shap...]
    ppermute x9 -> x3, starting transfers between devices: 8.82 us -> 4.47 us  [body(): packs.append(lax.ppermute(pack, 'cam', pattern))]
    pallas_call x1, Pallas kernels: 6.9 us -> 5.07 us  [update(): pl.pallas_call(functools.partial(update_kernel, groups), out_shape=(jax.S...]
    convert_element_type x2, other arithmetic: 0.08 us -> 1.37 us  [the longest x1 0.69 us: body(): sends = sends.astype(jnp.int32)]
  transfers between devices with their start and end apart: 9 -> 3, of which waited for: 4 -> 0; matrix products, arithmetic and copies ran while one was open for 7% -> 1% of each run, Pallas kernels for 46% -> 61%
where the time goes in v2:
time: 71.8 us; the launch traced here: 71.1 us
  Pallas kernels  61.5 us (86%)
  starting transfers between devices  4.47 us (6%)
  other arithmetic  2.47 us (3%)
  local copies, waits for them, and re-layouts  1.93 us (3%)
  between operations  0.79 us (1%)
    pallas_call x1, Pallas kernels, render(): pl.pallas_call(render_kernel, out_shape=(jax.ShapeDtypeStruct(targets.sha...  17.4 us
    pallas_call x1, Pallas kernels, return_home(): pl.pallas_call(functools.partial(return_kernel, owners, groups), out_shap...  15.6 us
    pallas_call x1, Pallas kernels, exchange(): pl.pallas_call(functools.partial(exchange_kernel, axis, count), out_shape...  10.8 us
    pallas_call x1, Pallas kernels, project(): pl.pallas_call(project_kernel, out_shape=jax.ShapeDtypeStruct(shape, F32)...  10.6 us
    pallas_call x1, Pallas kernels, update(): pl.pallas_call(functools.partial(update_kernel, groups), out_shape=(jax.S...  5.07 us
    ppermute x3, starting transfers between devices, body(): packs.append(lax.ppermute(pack, 'cam', pattern))  4.47 us
    pallas_call x1, Pallas kernels, divide(): pl.pallas_call(divide_kernel, out_shape=jax.ShapeDtypeStruct((owners, row...  2 us
    unnamed x16, local copies, waits for them, and re-layouts  1.73 us
  transfers between devices with their start and end apart: 3, of which 0 were waited for; matrix products, arithmetic and copies ran while one was open for 1% of the time, Pallas kernels for 61%

profile of v2, /device:TPU:1, one launch (start us, length us, event | category | flops | bytes accessed | tf_op | source)
XLA Modules:
  0.0 71.1 jit_solution(3282046266247162135)
XLA Ops:
  0.6 0.7 convert_element_type.10
  1.3 0.1 copy.20
  1.4 0.0 copy-start.5
  1.4 0.1 reshape.33
  1.5 0.6 copy-done.5
  2.1 0.0 copy-start.4
  2.1 0.0 copy-start.6
  2.1 1.1 %pad_maximum_fusion.refs_5_ = f32[984,128]{1,0:T(8,128)S(1)} fusion(f32[8,128]{1,0:T(8,128)S(1)} %pad_bitcast_fusion, f32[32,128]{1,0:T(8,128)S(1)} %bitcast.35, f32[472,128]{1,0:T(8,128)} %bitcast.33, f32[472,128]{1,0:T(8,128)} %bitcast.34), kind=kLoop, calls=%fused_computation | loop fusion | flops 377856 | bytes 1007616 | tf_op jit(solution)/shard_map/concatenate | solution.py:588
  3.2 0.0 copy-done.4
  3.3 0.0 copy-start
  3.3 2.1 %collective-permute-start.2 = (f32[984,128]{1,0:T(8,128)S(1)}, f32[984,128]{1,0:T(8,128)S(1)}, u32[]{:S(2)}, u32[]{:S(2)}) collective-permute-start(f32[984,128]{1,0:T(8,128)S(1)} %pad_maximum_fusion.refs_5_), channel_id=1, source_target_pairs={{24,0},{0,8},{8,16},{16,24},{25,1},{1,9},{9,17},{17,25},{26,2},{2,... | collective-permute-start | bytes 1511432 | tf_op jit(solution)/shard_map/ppermute | solution.py:592
  5.3 1.2 %collective-permute-start.1 = (f32[984,128]{1,0:T(8,128)S(1)}, f32[984,128]{1,0:T(8,128)S(1)}, u32[]{:S(2)}, u32[]{:S(2)}) collective-permute-start(f32[984,128]{1,0:T(8,128)S(1)} %pad_maximum_fusion.refs_5_), channel_id=1, source_target_pairs={{16,0},{24,8},{0,16},{8,24},{17,1},{25,9},{1,17},{9,25},{18,2},{26... | collective-permute-start | bytes 1511432 | tf_op jit(solution)/shard_map/ppermute | solution.py:592
  6.6 1.2 %collective-permute-start = (f32[984,128]{1,0:T(8,128)S(1)}, f32[984,128]{1,0:T(8,128)S(1)}, u32[]{:S(2)}, u32[]{:S(2)}) collective-permute-start(f32[984,128]{1,0:T(8,128)S(1)} %pad_maximum_fusion.refs_5_), channel_id=1, source_target_pairs={{8,0},{16,8},{24,16},{0,24},{9,1},{17,9},{25,17},{1,25},{10,2},{18... | collective-permute-start | bytes 1511432 | tf_op jit(solution)/shard_map/ppermute | solution.py:592
  7.7 0.0 copy-done.6
  7.7 0.7 copy.19.send_ref
  8.4 10.6 %project.1.received_ref = f32[8,36,128]{2,1,0:T(8,128)} custom-call(s32[2,1,8,2]{3,2,1,0:T(8,128)} %copy.19.send_ref, f32[32,128]{1,0:T(8,128)} %bitcast.36, f32[59,32,128]{2,1,0:T(8,128)} %bitcast.30), custom_call_target="tpu_custom_call" | custom-call | tf_op jit(solution)/shard_map/project/pallas_call | solution.py:97
  19.1 0.0 copy-done
  19.1 17.4 %render.1 = (f32[2,3,2,256]{3,2,1,0:T(2,128)}, f32[8,36,128]{2,1,0:T(8,128)}) custom-call(s32[2,2,8]{2,1,0:T(2,128)} %slot_ref.1, s32[2,2]{1,0:T(2,128)} %count_ref.1, f32[8,36,128]{2,1,0:T(8,128)} %project.1.received_ref, f32[2,3,2,256]{3,2,1,0:T(2,128)} %bitcast.40), custom_call_target="tpu_custom_call" | custom-call | flops 20000000000 | bytes 100000000 | tf_op jit(solution)/shard_map/render/pallas_call | solution.py:439
  36.5 15.6 %return_home.1.refs_3_ = f32[4,8,36,128]{3,2,1,0:T(8,128)} custom-call(f32[8,36,128]{2,1,0:T(8,128)} %get-tuple-element.12.x_ref), custom_call_target="tpu_custom_call" | custom-call | tf_op jit(solution)/shard_map/return_home/pallas_call | solution.py:221
  52.1 0.0 collective-permute-done.2.refs_8_
  52.1 0.0 copy-start.1
  52.1 0.0 collective-permute-done.1.refs_7_
  52.1 0.0 copy-start.2
  52.1 0.0 collective-permute-done.refs_6_
  52.1 0.0 copy-start.3
  52.2 0.7 maximum_convert_fusion.refs_0_
  52.9 0.0 copy-done.1
  52.9 0.2 copy-done.2
  53.1 0.2 copy-done.3
  53.3 5.1 %update.1 = (f32[59,32,128]{2,1,0:T(8,128)}, f32[59,8,128]{2,1,0:T(8,128)}, f32[59,8,128]{2,1,0:T(8,128)}, f32[8,60,128]{2,1,0:T(8,128)}) custom-call(s32[4,128]{1,0:T(4,128)} %maximum_convert_fusion.refs_0_, s32[1,8]{1,0:T(1,128)} %refs_1_.1, s32[1,8]{1,0:T(1,128)} %refs_2_.1, f32[4,8,36,128]{3,2,1,0:T(8,128)} %return_home.1.refs_3_, ...), custom_call_target="tpu_custom_call" | custom-call | tf_op jit(solution)/shard_map/update/pallas_call | solution.py:526
  58.3 10.8 %exchange_6.1.parent_ref = f32[8,60,128]{2,1,0:T(8,128)} custom-call(f32[8,60,128]{2,1,0:T(8,128)} %get-tuple-element.16.x_ref), custom_call_target="tpu_custom_call" | custom-call | tf_op jit(solution)/shard_map/exchange_6/pallas_call | solution.py:148
  69.1 2.0 %divide.1 = f32[8,59,2,128]{3,2,1,0:T(2,128)} custom-call(f32[8,60,128]{2,1,0:T(8,128)} %exchange_6.1.parent_ref), custom_call_target="tpu_custom_call" | custom-call | tf_op jit(solution)/shard_map/divide/pallas_call | solution.py:565
  (7 shorter events, 0.0 us)
Async XLA Ops:
  1.4 0.7 copy-start.5
  2.1 1.1 %copy-start.4 = (f32[2,16,128]{2,1,0:T(8,128)}, f32[2,16,128]{2,1,0:T(8,128)S(1)}, u32[]{:S(2)}) copy-start(f32[2,16,128]{2,1,0:T(8,128)S(1)} %pad.8.clone) | copy-start | bytes 49156
  2.1 5.6 %copy-start.6 = (s32[2,1,8,2]{2,3,1,0:T(2,128)S(1)}, s32[2,1,8,2]{2,3,1,0:T(2,128)}, u32[]{:S(2)}) copy-start(s32[2,1,8,2]{2,3,1,0:T(2,128)} %param.14) | copy-start | bytes 388
  3.3 15.8 %copy-start = (f32[984,128]{1,0:T(8,128)}, f32[984,128]{1,0:T(8,128)S(1)}, u32[]{:S(2)}) copy-start(f32[984,128]{1,0:T(8,128)S(1)} %pad_maximum_fusion.refs_5_) | copy-start | bytes 1511428
  3.3 48.8 %collective-permute-start.2 = (f32[984,128]{1,0:T(8,128)S(1)}, f32[984,128]{1,0:T(8,128)S(1)}, u32[]{:S(2)}, u32[]{:S(2)}) collective-permute-start(f32[984,128]{1,0:T(8,128)S(1)} %pad_maximum_fusion.refs_5_), channel_id=1, source_target_pairs={{24,0},{0,8},{8,16},{16,24},{25,1},{1,9},{9,17},{17,25},{26,2},{2,... | collective-permute-start | bytes 1511432 | tf_op jit(solution)/shard_map/ppermute | solution.py:592
  5.3 46.8 %collective-permute-start.1 = (f32[984,128]{1,0:T(8,128)S(1)}, f32[984,128]{1,0:T(8,128)S(1)}, u32[]{:S(2)}, u32[]{:S(2)}) collective-permute-start(f32[984,128]{1,0:T(8,128)S(1)} %pad_maximum_fusion.refs_5_), channel_id=1, source_target_pairs={{16,0},{24,8},{0,16},{8,24},{17,1},{25,9},{1,17},{9,25},{18,2},{26... | collective-permute-start | bytes 1511432 | tf_op jit(solution)/shard_map/ppermute | solution.py:592
  6.6 45.5 %collective-permute-start = (f32[984,128]{1,0:T(8,128)S(1)}, f32[984,128]{1,0:T(8,128)S(1)}, u32[]{:S(2)}, u32[]{:S(2)}) collective-permute-start(f32[984,128]{1,0:T(8,128)S(1)} %pad_maximum_fusion.refs_5_), channel_id=1, source_target_pairs={{8,0},{16,8},{24,16},{0,24},{9,1},{17,9},{25,17},{1,25},{10,2},{18... | collective-permute-start | bytes 1511432 | tf_op jit(solution)/shard_map/ppermute | solution.py:592
  52.1 0.8 %copy-start.1 = (f32[984,128]{1,0:T(8,128)}, f32[984,128]{1,0:T(8,128)S(1)}, u32[]{:S(2)}) copy-start(f32[984,128]{1,0:T(8,128)S(1)} %collective-permute-done.2.refs_8_) | copy-start | bytes 1511428
  52.1 0.9 %copy-start.2 = (f32[984,128]{1,0:T(8,128)}, f32[984,128]{1,0:T(8,128)S(1)}, u32[]{:S(2)}) copy-start(f32[984,128]{1,0:T(8,128)S(1)} %collective-permute-done.1.refs_7_) | copy-start | bytes 1511428
  52.1 1.1 %copy-start.3 = (f32[984,128]{1,0:T(8,128)}, f32[984,128]{1,0:T(8,128)S(1)}, u32[]{:S(2)}) copy-start(f32[984,128]{1,0:T(8,128)S(1)} %collective-permute-done.refs_6_) | copy-start | bytes 1511428

commit v3 on v2

--- a/solution.py
+++ b/solution.py
@@ -10,6 +10,7 @@
 
 TSIDE = 16
 PROJ = 9
+PAIR = 2
 LOSS_WEIGHT = 256.0
 RATE = 0.01
 BETA_FIRST = 0.9
@@ -47,7 +48,7 @@
     send_ref, matrix_ref, params_ref, out_ref, rows_ref, parcels, land, send_sems, recv_sems
 ):
     values, owned, _ = params_ref.shape
-    cameras, _, owners, cap = send_ref.shape
+    cameras, _, cap, owners = send_ref.shape
     me = lax.axis_index("dev")
     barrier = pltpu.get_barrier_semaphore()
     for step in range(1, owners):
@@ -62,7 +63,7 @@
     for owner in range(owners):
         for camera in range(cameras):
             for place in range(cap):
-                chosen = send_ref[camera, 0, owner, place]
+                chosen = send_ref[camera, 0, place, owner]
                 first = (camera * cap + place) * PROJ
                 parcels[owner, first : first + PROJ, :] = rows_ref[
                     chosen, camera * 16 : camera * 16 + PROJ, :
@@ -91,7 +92,7 @@
 
 
 def project(send_block, matrix, params):
-    cameras, _, owners, cap = send_block.shape
+    cameras, _, cap, owners = send_block.shape
     values, owned, splats = params.shape
     shape = (owners, cameras * cap * PROJ, splats)
     return pl.pallas_call(
@@ -299,43 +300,61 @@
         carry[...] = jnp.zeros(carry.shape, F32)
         picture[...] = jnp.zeros(picture.shape, F32)
 
-        def forward(position, _):
-            owner, index = entry_of(camera, tile, position)
-            part = lambda k: feats[owner, index, k : k + 1, :]
-            off_x = grid - part(0)
-            off_y = grid - part(1)
-            in_x = -(part(2) * off_x * off_x)
-            cross = -(part(3) * off_x)
-            in_y = part(5) - part(4) * off_y * off_y
-            for chunk in range(pixels // half):
+        def forward(pair, _):
+            places = [PAIR * pair + sub for sub in range(PAIR)]
+            alphas, logs, sums, shades = [], [], [], []
+            for place in places:
+                owner, index = entry_of(camera, tile, jnp.minimum(place, live - 1))
+                part = lambda k: feats[owner, index, k : k + 1, :]
+                off_x = grid - part(0)
+                off_y = grid - part(1)
+                in_x = -(part(2) * off_x * off_x)
+                cross = -(part(3) * off_x)
+                faint = jnp.where(place < live, part(5), -1e30)
+                in_y = faint - part(4) * off_y * off_y
+                for chunk in range(pixels // half):
+                    lines = []
+                    for line in range(chunk * per_chunk, (chunk + 1) * per_chunk):
+                        lines.append(
+                            in_x + (in_y[line : line + 1] + cross * off_y[line : line + 1])
+                        )
+                    alpha = jnp.exp2(jnp.concatenate(lines, axis=0))
+                    log_keep = jnp.log2(1.0 - alpha)
+                    alphas.append(alpha)
+                    logs.append(log_keep)
+                    sums.append(dot32(jnp.concatenate(split2(log_keep), axis=1), before[...]))
+                colour_high, colour_low = split2(feats[owner, index, 8:16, :])
+                colour_high = colour_high.astype(F32)
+                colour_low = colour_low.astype(F32)
+                shades.append(
+                    jnp.concatenate(
+                        [
+                            jnp.concatenate([colour_high, colour_low], axis=0),
+                            jnp.concatenate([colour_high, pad_rows], axis=0),
+                        ],
+                        axis=1,
+                    ).astype(BF16)
+                )
+            chunks = pixels // half
+            for chunk in range(chunks):
                 where = slice(chunk * half, (chunk + 1) * half)
-                lines = []
-                for line in range(chunk * per_chunk, (chunk + 1) * per_chunk):
-                    lines.append(in_x + (in_y[line : line + 1] + cross * off_y[line : line + 1]))
-                alpha = jnp.exp2(jnp.concatenate(lines, axis=0))
-                log_keep = jnp.log2(1.0 - alpha)
-                summed = dot32(jnp.concatenate(split2(log_keep), axis=1), before[...])
                 held = carry[where, :]
-                weight = alpha * jnp.exp2(summed[:, :splats] + held)
-                carry[where, :] = held + summed[:, splats:]
-                weights[position, where, :] = weight
-                pairs[position, where, :] = jnp.concatenate(split2(weight), axis=1)
-                ratios[position, where, :] = alpha * jnp.exp2(-log_keep)
-            colour_high, colour_low = split2(feats[owner, index, 8:16, :])
-            colour_high = colour_high.astype(F32)
-            colour_low = colour_low.astype(F32)
-            shades = jnp.concatenate(
-                [
-                    jnp.concatenate([colour_high, colour_low], axis=0),
-                    jnp.concatenate([colour_high, pad_rows], axis=0),
-                ],
-                axis=1,
-            ).astype(BF16)
-            drawn = dot32(shades, pairs[position], (((1,), (1,)), ((), ())))
-            picture[...] += drawn[:8] + drawn[8:]
+                drawn = jnp.zeros((16, half), F32)
+                for sub, place in enumerate(places):
+                    at = sub * chunks + chunk
+                    weight = alphas[at] * jnp.exp2(sums[at][:, :splats] + held)
+                    held = held + sums[at][:, splats:]
+                    both = jnp.concatenate(split2(weight), axis=1)
+                    weights[place, where, :] = weight
+                    pairs[place, where, :] = both
+                    ratios[place, where, :] = alphas[at] * jnp.exp2(-logs[at])
+                    drawn += dot32(shades[sub], both, (((1,), (1,)), ((), ())))
+                carry[where, :] = held
+                picture[:, where] += drawn[:8] + drawn[8:]
             return 0
 
-        lax.fori_loop(0, live, forward, 0)
+        steps = (live + PAIR - 1) // PAIR
+        lax.fori_loop(0, steps, forward, 0)
         for k in range(3):
             colour = picture[k : k + 1, :]
             image_ref[camera, k, pl.ds(tile, 1), :] = colour
@@ -353,57 +372,76 @@
         carry[...] = jnp.zeros(carry.shape, F32)
 
         def backward(reverse, _):
-            position = live - 1 - reverse
-            owner, index = entry_of(camera, tile, position)
-            part = lambda k: feats[owner, index, k : k + 1, :]
-            off_x = grid - part(0)
-            off_y = grid - part(1)
-            colour_high, colour_low = split2(feats[owner, index, 8:16, :])
-            colour_high = colour_high.astype(F32)
-            shades = jnp.concatenate(
-                [colour_high, colour_high, colour_low.astype(F32), jnp.zeros((half - 24, splats), F32)],
-                axis=0,
-            ).astype(BF16)
-            total0 = jnp.zeros((TSIDE, splats), F32)
-            total1 = jnp.zeros((TSIDE, splats), F32)
-            total2 = jnp.zeros((TSIDE, splats), F32)
-            for chunk in range(pixels // half):
+            places = [PAIR * (steps - 1 - reverse) + PAIR - 1 - sub for sub in range(PAIR)]
+            chunks = pixels // half
+            spots, offsets, shaded, sums = [], [], [], []
+            for place in places:
+                owner, index = entry_of(camera, tile, jnp.minimum(place, live - 1))
+                spots.append((owner, index))
+                offsets.append(
+                    (grid - feats[owner, index, 0:1, :], grid - feats[owner, index, 1:2, :])
+                )
+                colour_high, colour_low = split2(feats[owner, index, 8:16, :])
+                colour_high = colour_high.astype(F32)
+                shades = jnp.concatenate(
+                    [
+                        colour_high,
+                        colour_high,
+                        colour_low.astype(F32),
+                        jnp.zeros((half - 24, splats), F32),
+                    ],
+                    axis=0,
+                ).astype(BF16)
+                for chunk in range(chunks):
+                    where = slice(chunk * half, (chunk + 1) * half)
+                    piece = dot32(cot_cols[where, :], shades) * weights[place, where, :]
+                    shaded.append(piece)
+                    sums.append(dot32(jnp.concatenate(split2(piece), axis=1), after_tri[...]))
+            totals = [[jnp.zeros((TSIDE, splats), F32)] * 3 for _ in places]
+            for chunk in range(chunks):
                 where = slice(chunk * half, (chunk + 1) * half)
-                shade = dot32(cot_cols[where, :], shades)
-                shaded = shade * weights[position, where, :]
-                summed = dot32(jnp.concatenate(split2(shaded), axis=1), after_tri[...])
                 held = carry[where, :]
-                carry[where, :] = held + summed[:, splats:]
-                pull = shaded - (summed[:, :splats] + held) * ratios[position, where, :]
-                for line in range(per_chunk):
-                    height = off_y[chunk * per_chunk + line : chunk * per_chunk + line + 1]
-                    piece = pull[line * TSIDE : (line + 1) * TSIDE]
-                    lifted = piece * height
-                    total0 += piece
-                    total1 += lifted
-                    total2 += lifted * height
+                for sub, place in enumerate(places):
+                    at = sub * chunks + chunk
+                    pull = shaded[at] - (sums[at][:, :splats] + held) * ratios[place, where, :]
+                    held = held + sums[at][:, splats:]
+                    total0, total1, total2 = totals[sub]
+                    off_y = offsets[sub][1]
+                    for line in range(per_chunk):
+                        height = off_y[chunk * per_chunk + line : chunk * per_chunk + line + 1]
+                        piece = pull[line * TSIDE : (line + 1) * TSIDE]
+                        lifted = piece * height
+                        total0 += piece
+                        total1 += lifted
+                        total2 += lifted * height
+                    totals[sub] = [total0, total1, total2]
+                carry[where, :] = held
             sum_of = lambda value: jnp.sum(value, axis=0, keepdims=True)
-            wide = total0 * off_x
-            moments = jnp.concatenate(
-                [
-                    sum_of(total0),
-                    sum_of(wide),
-                    sum_of(total1),
-                    sum_of(wide * off_x),
-                    sum_of(total1 * off_x),
-                    sum_of(total2),
-                    jnp.zeros((2, splats), F32),
-                ],
-                axis=0,
-            )
-            tinted = dot32(cot_rows[...], pairs[position])
-            grads[owner, index, 0:8, :] += moments
-            grads[owner, index, 8:16, :] += (
-                tinted[:8, :splats] + tinted[8:, :splats] + tinted[:8, splats:]
-            )
+            for sub, place in enumerate(places):
+                owner, index = spots[sub]
+                total0, total1, total2 = totals[sub]
+                off_x = offsets[sub][0]
+                wide = total0 * off_x
+                moments = jnp.concatenate(
+                    [
+                        sum_of(total0),
+                        sum_of(wide),
+                        sum_of(total1),
+                        sum_of(wide * off_x),
+                        sum_of(total1 * off_x),
+                        sum_of(total2),
+                        jnp.zeros((2, splats), F32),
+                    ],
+                    axis=0,
+                )
+                tinted = dot32(cot_rows[...], pairs[place])
+                grads[owner, index, 0:8, :] += moments
+                grads[owner, index, 8:16, :] += (
+                    tinted[:8, :splats] + tinted[8:, :splats] + tinted[:8, splats:]
+                )
             return 0
 
-        lax.fori_loop(0, live, backward, 0)
+        lax.fori_loop(0, steps, backward, 0)
         return 0
 
     lax.fori_loop(0, cameras * tiles, tile_step, 0)
@@ -436,6 +474,7 @@
     cameras, tiles, depth = slots.shape
     pixels = targets.shape[-1]
     cap = rows // (PROJ * cameras)
+    depth = -(-depth // PAIR) * PAIR
     return pl.pallas_call(
         render_kernel,
         out_shape=(
@@ -466,9 +505,17 @@
 
 
 def update_kernel(groups, *refs):
-    send_ref, split_ref, live_ref, back_ref, params_ref = refs[:5]
-    packs = refs[5 : 5 + groups]
-    params_out, first_out, second_out, parent_out, table, slopes = refs[5 + groups :]
+    send_ref, split_ref, live_ref, back_ref, params_hbm = refs[:5]
+    packs_hbm = refs[5 : 5 + groups]
+    (params_out, first_out, second_out, parent_out) = refs[5 + groups : 9 + groups]
+    table, slopes, params_ref, packs, arrivals = refs[9 + groups :]
+    loads = [
+        pltpu.make_async_copy(packs_hbm[turn], packs.at[turn], arrivals.at[turn])
+        for turn in range(groups)
+    ]
+    loads.append(pltpu.make_async_copy(params_hbm, params_ref, arrivals.at[groups]))
+    for load in loads:
+        load.start()
     me = lax.axis_index("cam")
     owners, rows = back_ref.shape[1:3]
     values, share, splats = first_out.shape
@@ -479,15 +526,17 @@
         for owner in range(owners):
             for camera in range(cameras):
                 for place in range(cap):
-                    block = send_ref[turn, (camera * owners + owner) * cap + place]
+                    block = send_ref[turn, (camera * cap + place) * owners + owner]
                     first = (camera * cap + place) * PROJ
                     into = (turn * cameras + camera) * 16
                     table[block, into : into + PROJ, :] += back_ref[
                         turn, owner, first : first + PROJ, :
                     ]
     held = values * share
+    for load in loads:
+        load.wait()
     stacked = jnp.concatenate(
-        [pack[2 * held : 2 * held + 16 * cameras, :] for pack in packs], axis=0
+        [packs[turn, 2 * held : 2 * held + 16 * cameras, :] for turn in range(groups)], axis=0
     )
     matrix_high, matrix_low = split2(stacked.T[: -(-values // 16) * 16])
     both = jnp.concatenate([matrix_high, matrix_low], axis=1)
@@ -497,7 +546,7 @@
             high, low = split2(table[base + place])
             gradient = dot32(both, jnp.concatenate([high, high], axis=0)) + dot32(matrix_high, low)
             slopes[:, place, :] = gradient[:values]
-        pack = packs[turn]
+        pack = packs.at[turn]
         for start in range(0, values, 8):
             end = min(values, start + 8)
             size = (end - start, share, splats)
@@ -531,11 +580,14 @@
             moments,
             jax.ShapeDtypeStruct((split_block.shape[1], values + 1, splats), F32),
         ),
-        in_specs=[SMEM, SMEM, SMEM] + [VMEM] * (2 + groups),
+        in_specs=[SMEM, SMEM, SMEM, VMEM] + [pl.BlockSpec(memory_space=pl.ANY)] * (1 + groups),
         out_specs=(VMEM,) * 4,
         scratch_shapes=[
             pltpu.VMEM((owned, groups * 16 * cameras, splats), F32),
             pltpu.VMEM((values, share, splats), F32),
+            pltpu.VMEM(params.shape, F32),
+            pltpu.VMEM((groups,) + packs[0].shape, F32),
+            pltpu.SemaphoreType.DMA((groups + 1,)),
         ],
         compiler_params=pltpu.CompilerParams(vmem_limit_bytes=BIG),
         name="update",
@@ -582,6 +634,7 @@
     share = moment_first.shape[2]
     matrix = jnp.pad(cam_proj, ((0, 0), (0, 16 - rows), (0, 128 - values)))
     matrix = matrix.reshape(cameras * 16, 128)
+    send_block = send_block.transpose(0, 1, 3, 2)
     numbers = send_block.astype(F32).reshape(-1)
     numbers = jnp.pad(numbers, (0, -numbers.size % 1024)).reshape(-1, 128)
     by_value = lambda moment: moment[0, 0].transpose(1, 0, 2).reshape(values * share, splats)

time: 71.8 us -> 67.4 us (0.939)
  Pallas kernels: 61.5 us -> 59.1 us
  local copies, waits for them, and re-layouts: 1.93 us -> 0.52 us
    pallas_call x1, Pallas kernels: 17.4 us -> 12.7 us  [render(): pl.pallas_call(render_kernel, out_shape=(jax.ShapeDtypeStruct(targets.sha...]
    pallas_call x1, Pallas kernels: 10.8 us -> 12.2 us  [exchange(): pl.pallas_call(functools.partial(exchange_kernel, axis, count), out_shape...]
    unnamed x16 -> x13, local copies, waits for them, and re-layouts: 1.73 us -> 0.41 us
  transfers between devices with their start and end apart: 3 -> 3, of which waited for: 0 -> 0; matrix products, arithmetic and copies ran while one was open for 1% -> 0% of each run, Pallas kernels for 61% -> 58%
where the time goes in v3:
time: 67.4 us
  Pallas kernels  59.1 us (88%)
  starting transfers between devices  4.47 us (7%)
  other arithmetic  2.47 us (4%)
  between operations  0.8 us (1%)
    pallas_call x1, Pallas kernels, return_home(): pl.pallas_call(functools.partial(return_kernel, owners, groups), out_shap...  15.9 us
    pallas_call x1, Pallas kernels, render(): pl.pallas_call(render_kernel, out_shape=(jax.ShapeDtypeStruct(targets.sha...  12.7 us
    pallas_call x1, Pallas kernels, exchange(): pl.pallas_call(functools.partial(exchange_kernel, axis, count), out_shape...  12.2 us
    pallas_call x1, Pallas kernels, project(): pl.pallas_call(project_kernel, out_shape=jax.ShapeDtypeStruct(shape, F32)...  10.6 us
    pallas_call x1, Pallas kernels, update(): pl.pallas_call(functools.partial(update_kernel, groups), out_shape=(jax.S...  5.69 us
    ppermute x3, starting transfers between devices, body(): packs.append(lax.ppermute(pack, 'cam', pattern))  4.47 us
    pallas_call x1, Pallas kernels, divide(): pl.pallas_call(divide_kernel, out_shape=jax.ShapeDtypeStruct((owners, row...  2 us
  transfers between devices with their start and end apart: 3, of which 0 were waited for; matrix products, arithmetic and copies ran while one was open for 0% of the time, Pallas kernels for 58%

profile of v3, /device:TPU:1, one launch (start us, length us, event | category | flops | bytes accessed | tf_op | source)
XLA Modules:
  0.0 67.4 jit_solution(6217639838899184339)
XLA Ops:
  0.6 0.0 copy-start.5
  0.6 0.7 %bitcast_convert_fusion = f32[2,1,2,8]{3,2,1,0:T(2,128)S(1)} fusion(s32[2,1,8,2]{2,3,1,0:T(2,128)} %param.14), kind=kLoop, calls=%fused_computation.5 | loop fusion | flops 32 | bytes 256 | tf_op jit(solution)/shard_map/convert_element_type | solution.py:638
  1.3 0.1 reshape.33
  1.4 0.0 copy-done.5
  1.4 0.0 copy-start.4
  1.5 1.1 %pad_maximum_fusion.refs_5_ = f32[984,128]{1,0:T(8,128)S(1)} fusion(f32[8,128]{1,0:T(8,128)S(1)} %pad_bitcast_fusion, f32[32,128]{1,0:T(8,128)S(1)} %bitcast.33, f32[472,128]{1,0:T(8,128)} %bitcast.31, f32[472,128]{1,0:T(8,128)} %bitcast.32), kind=kLoop, calls=%fused_computation | loop fusion | flops 377856 | bytes 1007616 | tf_op jit(solution)/shard_map/concatenate | solution.py:641
  2.6 0.0 copy-done.4
  2.6 0.0 copy-start
  2.6 2.1 %collective-permute-start.2 = (f32[984,128]{1,0:T(8,128)S(1)}, f32[984,128]{1,0:T(8,128)S(1)}, u32[]{:S(2)}, u32[]{:S(2)}) collective-permute-start(f32[984,128]{1,0:T(8,128)S(1)} %pad_maximum_fusion.refs_5_), channel_id=1, source_target_pairs={{24,0},{0,8},{8,16},{16,24},{25,1},{1,9},{9,17},{17,25},{26,2},{2,... | collective-permute-start | bytes 1511432 | tf_op jit(solution)/shard_map/ppermute | solution.py:645
  4.7 1.2 %collective-permute-start.1 = (f32[984,128]{1,0:T(8,128)S(1)}, f32[984,128]{1,0:T(8,128)S(1)}, u32[]{:S(2)}, u32[]{:S(2)}) collective-permute-start(f32[984,128]{1,0:T(8,128)S(1)} %pad_maximum_fusion.refs_5_), channel_id=1, source_target_pairs={{16,0},{24,8},{0,16},{8,24},{17,1},{25,9},{1,17},{9,25},{18,2},{26... | collective-permute-start | bytes 1511432 | tf_op jit(solution)/shard_map/ppermute | solution.py:645
  5.9 1.2 %collective-permute-start = (f32[984,128]{1,0:T(8,128)S(1)}, f32[984,128]{1,0:T(8,128)S(1)}, u32[]{:S(2)}, u32[]{:S(2)}) collective-permute-start(f32[984,128]{1,0:T(8,128)S(1)} %pad_maximum_fusion.refs_5_), channel_id=1, source_target_pairs={{8,0},{16,8},{24,16},{0,24},{9,1},{17,9},{25,17},{1,25},{10,2},{18... | collective-permute-start | bytes 1511432 | tf_op jit(solution)/shard_map/ppermute | solution.py:645
  7.1 10.6 %project.1.received_ref = f32[8,36,128]{2,1,0:T(8,128)} custom-call(s32[2,1,2,8]{3,2,1,0:T(2,128)} %bitcast.35, f32[32,128]{1,0:T(8,128)} %bitcast.34, f32[59,32,128]{2,1,0:T(8,128)} %bitcast.28), custom_call_target="tpu_custom_call" | custom-call | tf_op jit(solution)/shard_map/project/pallas_call | solution.py:98
  17.7 0.0 copy-done
  17.7 12.7 %render.1 = (f32[2,3,2,256]{3,2,1,0:T(2,128)}, f32[8,36,128]{2,1,0:T(8,128)}) custom-call(s32[2,2,8]{2,1,0:T(2,128)} %slot_ref.1, s32[2,2]{1,0:T(2,128)} %count_ref.1, f32[8,36,128]{2,1,0:T(8,128)} %project.1.received_ref, f32[2,3,2,256]{3,2,1,0:T(2,128)} %bitcast.39), custom_call_target="tpu_custom_call" | custom-call | flops 20000000000 | bytes 100000000 | tf_op jit(solution)/shard_map/render/pallas_call | solution.py:478
  30.4 15.9 %return_home.1.refs_3_ = f32[4,8,36,128]{3,2,1,0:T(8,128)} custom-call(f32[8,36,128]{2,1,0:T(8,128)} %get-tuple-element.12.x_ref), custom_call_target="tpu_custom_call" | custom-call | tf_op jit(solution)/shard_map/return_home/pallas_call | solution.py:222
  46.3 0.0 collective-permute-done.2.refs_8_
  46.3 0.0 copy-start.1
  46.3 0.0 collective-permute-done.1.refs_7_
  46.3 0.0 copy-start.2
  46.4 0.0 collective-permute-done.refs_6_
  46.4 0.0 copy-start.3
  46.4 0.7 %maximum_convert_fusion.refs_0_ = s32[4,128]{1,0:T(4,128)} fusion(f32[1,128]{1,0:T(1,128)S(1)} %slice.22, f32[1,128]{1,0:T(1,128)S(1)} %slice.21, f32[1,128]{1,0:T(1,128)S(1)} %slice.20, f32[1,128]{1,0:T(1,128)S(1)} %fusion), kind=kLoop, calls=%fused_computation.3 | loop fusion | flops 2048 | bytes 4096 | tf_op jit(solution)/shard_map/convert_element_type | solution.py:649
  47.1 0.0 copy-done.1
  47.1 0.2 copy-done.2
  47.3 0.2 copy-done.3
  47.5 5.7 %update.1 = (f32[59,32,128]{2,1,0:T(8,128)}, f32[59,8,128]{2,1,0:T(8,128)}, f32[59,8,128]{2,1,0:T(8,128)}, f32[8,60,128]{2,1,0:T(8,128)}) custom-call(s32[4,128]{1,0:T(4,128)} %maximum_convert_fusion.refs_0_, s32[1,8]{1,0:T(1,128)} %refs_1_.1, s32[1,8]{1,0:T(1,128)} %refs_2_.1, f32[4,8,36,128]{3,2,1,0:T(8,128)} %return_home.1.refs_3_, ...), custom_call_target="tpu_custom_call" | custom-call | tf_op jit(solution)/shard_map/update/pallas_call | solution.py:575
  53.2 12.2 %exchange_6.1.parent_ref = f32[8,60,128]{2,1,0:T(8,128)} custom-call(f32[8,60,128]{2,1,0:T(8,128)} %get-tuple-element.16.x_ref), custom_call_target="tpu_custom_call" | custom-call | tf_op jit(solution)/shard_map/exchange_6/pallas_call | solution.py:149
  65.4 2.0 %divide.1 = f32[8,59,2,128]{3,2,1,0:T(2,128)} custom-call(f32[8,60,128]{2,1,0:T(8,128)} %exchange_6.1.parent_ref), custom_call_target="tpu_custom_call" | custom-call | tf_op jit(solution)/shard_map/divide/pallas_call | solution.py:617
  (7 shorter events, 0.0 us)
Async XLA Ops:
  0.6 0.8 %copy-start.5 = (f32[2,9,59]{2,0,1:T(2,128)S(1)}, f32[2,9,59]{2,0,1:T(2,128)}, u32[]{:S(2)}) copy-start(f32[2,9,59]{2,0,1:T(2,128)} %param.13) | copy-start | bytes 12748
  1.4 1.1 %copy-start.4 = (f32[2,16,128]{2,1,0:T(8,128)}, f32[2,16,128]{2,1,0:T(8,128)S(1)}, u32[]{:S(2)}) copy-start(f32[2,16,128]{2,1,0:T(8,128)S(1)} %pad.8.clone) | copy-start | bytes 49156
  2.6 15.1 %copy-start = (f32[984,128]{1,0:T(8,128)}, f32[984,128]{1,0:T(8,128)S(1)}, u32[]{:S(2)}) copy-start(f32[984,128]{1,0:T(8,128)S(1)} %pad_maximum_fusion.refs_5_) | copy-start | bytes 1511428
  2.6 43.7 %collective-permute-start.2 = (f32[984,128]{1,0:T(8,128)S(1)}, f32[984,128]{1,0:T(8,128)S(1)}, u32[]{:S(2)}, u32[]{:S(2)}) collective-permute-start(f32[984,128]{1,0:T(8,128)S(1)} %pad_maximum_fusion.refs_5_), channel_id=1, source_target_pairs={{24,0},{0,8},{8,16},{16,24},{25,1},{1,9},{9,17},{17,25},{26,2},{2,... | collective-permute-start | bytes 1511432 | tf_op jit(solution)/shard_map/ppermute | solution.py:645
  4.7 41.7 %collective-permute-start.1 = (f32[984,128]{1,0:T(8,128)S(1)}, f32[984,128]{1,0:T(8,128)S(1)}, u32[]{:S(2)}, u32[]{:S(2)}) collective-permute-start(f32[984,128]{1,0:T(8,128)S(1)} %pad_maximum_fusion.refs_5_), channel_id=1, source_target_pairs={{16,0},{24,8},{0,16},{8,24},{17,1},{25,9},{1,17},{9,25},{18,2},{26... | collective-permute-start | bytes 1511432 | tf_op jit(solution)/shard_map/ppermute | solution.py:645
  5.9 40.5 %collective-permute-start = (f32[984,128]{1,0:T(8,128)S(1)}, f32[984,128]{1,0:T(8,128)S(1)}, u32[]{:S(2)}, u32[]{:S(2)}) collective-permute-start(f32[984,128]{1,0:T(8,128)S(1)} %pad_maximum_fusion.refs_5_), channel_id=1, source_target_pairs={{8,0},{16,8},{24,16},{0,24},{9,1},{17,9},{25,17},{1,25},{10,2},{18... | collective-permute-start | bytes 1511432 | tf_op jit(solution)/shard_map/ppermute | solution.py:645
  46.3 0.8 %copy-start.1 = (f32[984,128]{1,0:T(8,128)}, f32[984,128]{1,0:T(8,128)S(1)}, u32[]{:S(2)}) copy-start(f32[984,128]{1,0:T(8,128)S(1)} %collective-permute-done.2.refs_8_) | copy-start | bytes 1511428
  46.3 0.9 %copy-start.2 = (f32[984,128]{1,0:T(8,128)}, f32[984,128]{1,0:T(8,128)S(1)}, u32[]{:S(2)}) copy-start(f32[984,128]{1,0:T(8,128)S(1)} %collective-permute-done.1.refs_7_) | copy-start | bytes 1511428
  46.4 1.1 %copy-start.3 = (f32[984,128]{1,0:T(8,128)}, f32[984,128]{1,0:T(8,128)S(1)}, u32[]{:S(2)}) copy-start(f32[984,128]{1,0:T(8,128)S(1)} %collective-permute-done.refs_6_) | copy-start | bytes 1511428

commit v4 on v3

--- a/solution.py
+++ b/solution.py
@@ -55,11 +55,13 @@
         pl.semaphore_signal(
             barrier, inc=1, device_id={"dev": lax.rem(me + step, owners)}, device_id_type=MESH
         )
-    matrix = matrix_ref[:, :values]
+    matrix_high, matrix_low = split2(matrix_ref[:, :values])
+    both = jnp.concatenate([matrix_high, matrix_low], axis=0)
+    lines = matrix_ref.shape[0]
     for block in range(owned):
-        rows_ref[block] = jnp.dot(
-            matrix, params_ref[:, block, :], precision=HIGHEST, preferred_element_type=F32
-        )
+        high, low = split2(params_ref[:, block, :])
+        wide = dot32(both, high)
+        rows_ref[block] = wide[:lines] + (wide[lines:] + dot32(matrix_high, low))
     for owner in range(owners):
         for camera in range(cameras):
             for place in range(cap):
@@ -505,17 +507,9 @@
 
 
 def update_kernel(groups, *refs):
-    send_ref, split_ref, live_ref, back_ref, params_hbm = refs[:5]
-    packs_hbm = refs[5 : 5 + groups]
-    (params_out, first_out, second_out, parent_out) = refs[5 + groups : 9 + groups]
-    table, slopes, params_ref, packs, arrivals = refs[9 + groups :]
-    loads = [
-        pltpu.make_async_copy(packs_hbm[turn], packs.at[turn], arrivals.at[turn])
-        for turn in range(groups)
-    ]
-    loads.append(pltpu.make_async_copy(params_hbm, params_ref, arrivals.at[groups]))
-    for load in loads:
-        load.start()
+    send_ref, split_ref, live_ref, back_ref, params_ref = refs[:5]
+    packs = refs[5 : 5 + groups]
+    params_out, first_out, second_out, parent_out, table, slopes = refs[5 + groups :]
     me = lax.axis_index("cam")
     owners, rows = back_ref.shape[1:3]
     values, share, splats = first_out.shape
@@ -533,10 +527,8 @@
                         turn, owner, first : first + PROJ, :
                     ]
     held = values * share
-    for load in loads:
-        load.wait()
     stacked = jnp.concatenate(
-        [packs[turn, 2 * held : 2 * held + 16 * cameras, :] for turn in range(groups)], axis=0
+        [pack[2 * held : 2 * held + 16 * cameras, :] for pack in packs], axis=0
     )
     matrix_high, matrix_low = split2(stacked.T[: -(-values // 16) * 16])
     both = jnp.concatenate([matrix_high, matrix_low], axis=1)
@@ -546,7 +538,7 @@
             high, low = split2(table[base + place])
             gradient = dot32(both, jnp.concatenate([high, high], axis=0)) + dot32(matrix_high, low)
             slopes[:, place, :] = gradient[:values]
-        pack = packs.at[turn]
+        pack = packs[turn]
         for start in range(0, values, 8):
             end = min(values, start + 8)
             size = (end - start, share, splats)
@@ -580,14 +572,11 @@
             moments,
             jax.ShapeDtypeStruct((split_block.shape[1], values + 1, splats), F32),
         ),
-        in_specs=[SMEM, SMEM, SMEM, VMEM] + [pl.BlockSpec(memory_space=pl.ANY)] * (1 + groups),
+        in_specs=[SMEM, SMEM, SMEM] + [VMEM] * (2 + groups),
         out_specs=(VMEM,) * 4,
         scratch_shapes=[
             pltpu.VMEM((owned, groups * 16 * cameras, splats), F32),
             pltpu.VMEM((values, share, splats), F32),
-            pltpu.VMEM(params.shape, F32),
-            pltpu.VMEM((groups,) + packs[0].shape, F32),
-            pltpu.SemaphoreType.DMA((groups + 1,)),
         ],
         compiler_params=pltpu.CompilerParams(vmem_limit_bytes=BIG),
         name="update",

time: 67.4 us -> 68.3 us (1.013)
  Pallas kernels: 59.1 us -> 59.8 us
    pallas_call x1, Pallas kernels: 12.2 us -> 10.6 us  [exchange(): pl.pallas_call(functools.partial(exchange_kernel, axis, count), out_shape...]
    pallas_call x1, Pallas kernels: 15.9 us -> 17.3 us  [return_home(): pl.pallas_call(functools.partial(return_kernel, owners, groups), out_shap...]
    pallas_call x1, Pallas kernels: 12.7 us -> 13.7 us  [render(): pl.pallas_call(render_kernel, out_shape=(jax.ShapeDtypeStruct(targets.sha...]
  transfers between devices with their start and end apart: 3 -> 3, of which waited for: 0 -> 0; matrix products, arithmetic and copies ran while one was open for 0% -> 0% of each run, Pallas kernels for 58% -> 62%
where the time goes in v4:
time: 68.3 us; the launch traced here: 68.1 us
  Pallas kernels  59.8 us (88%)
  starting transfers between devices  4.47 us (7%)
  other arithmetic  2.47 us (4%)
  between operations  0.79 us (1%)
    pallas_call x1, Pallas kernels, return_home(): pl.pallas_call(functools.partial(return_kernel, owners, groups), out_shap...  17.3 us
    pallas_call x1, Pallas kernels, render(): pl.pallas_call(render_kernel, out_shape=(jax.ShapeDtypeStruct(targets.sha...  13.7 us
    pallas_call x1, Pallas kernels, project(): pl.pallas_call(project_kernel, out_shape=jax.ShapeDtypeStruct(shape, F32)...  11.2 us
    pallas_call x1, Pallas kernels, exchange(): pl.pallas_call(functools.partial(exchange_kernel, axis, count), out_shape...  10.6 us
    pallas_call x1, Pallas kernels, update(): pl.pallas_call(functools.partial(update_kernel, groups), out_shape=(jax.S...  5.07 us
    ppermute x3, starting transfers between devices, body(): packs.append(lax.ppermute(pack, 'cam', pattern))  4.47 us
    pallas_call x1, Pallas kernels, divide(): pl.pallas_call(divide_kernel, out_shape=jax.ShapeDtypeStruct((owners, row...  2 us
  transfers between devices with their start and end apart: 3, of which 0 were waited for; matrix products, arithmetic and copies ran while one was open for 0% of the time, Pallas kernels for 62%

profile of v4, /device:TPU:1, one launch (start us, length us, event | category | flops | bytes accessed | tf_op | source)
XLA Modules:
  0.0 68.1 jit_solution(11828858295889543432)
XLA Ops:
  0.6 0.0 copy-start.5
  0.6 0.7 %bitcast_convert_fusion = f32[2,1,2,8]{3,2,1,0:T(2,128)S(1)} fusion(s32[2,1,8,2]{2,3,1,0:T(2,128)} %param.14), kind=kLoop, calls=%fused_computation.5 | loop fusion | flops 32 | bytes 256 | tf_op jit(solution)/shard_map/convert_element_type | solution.py:627
  1.3 0.1 reshape.33
  1.4 0.0 copy-done.5
  1.4 0.0 copy-start.4
  1.5 1.1 %pad_maximum_fusion.refs_5_ = f32[984,128]{1,0:T(8,128)S(1)} fusion(f32[8,128]{1,0:T(8,128)S(1)} %pad_bitcast_fusion, f32[32,128]{1,0:T(8,128)S(1)} %bitcast.33, f32[472,128]{1,0:T(8,128)} %bitcast.31, f32[472,128]{1,0:T(8,128)} %bitcast.32), kind=kLoop, calls=%fused_computation | loop fusion | flops 377856 | bytes 1007616 | tf_op jit(solution)/shard_map/concatenate | solution.py:630
  2.6 0.0 copy-done.4
  2.6 0.0 copy-start
  2.6 2.1 %collective-permute-start.2 = (f32[984,128]{1,0:T(8,128)S(1)}, f32[984,128]{1,0:T(8,128)S(1)}, u32[]{:S(2)}, u32[]{:S(2)}) collective-permute-start(f32[984,128]{1,0:T(8,128)S(1)} %pad_maximum_fusion.refs_5_), channel_id=1, source_target_pairs={{24,0},{0,8},{8,16},{16,24},{25,1},{1,9},{9,17},{17,25},{26,2},{2,... | collective-permute-start | bytes 1511432 | tf_op jit(solution)/shard_map/ppermute | solution.py:634
  4.7 1.2 %collective-permute-start.1 = (f32[984,128]{1,0:T(8,128)S(1)}, f32[984,128]{1,0:T(8,128)S(1)}, u32[]{:S(2)}, u32[]{:S(2)}) collective-permute-start(f32[984,128]{1,0:T(8,128)S(1)} %pad_maximum_fusion.refs_5_), channel_id=1, source_target_pairs={{16,0},{24,8},{0,16},{8,24},{17,1},{25,9},{1,17},{9,25},{18,2},{26... | collective-permute-start | bytes 1511432 | tf_op jit(solution)/shard_map/ppermute | solution.py:634
  5.9 1.2 %collective-permute-start = (f32[984,128]{1,0:T(8,128)S(1)}, f32[984,128]{1,0:T(8,128)S(1)}, u32[]{:S(2)}, u32[]{:S(2)}) collective-permute-start(f32[984,128]{1,0:T(8,128)S(1)} %pad_maximum_fusion.refs_5_), channel_id=1, source_target_pairs={{8,0},{16,8},{24,16},{0,24},{9,1},{17,9},{25,17},{1,25},{10,2},{18... | collective-permute-start | bytes 1511432 | tf_op jit(solution)/shard_map/ppermute | solution.py:634
  7.1 11.2 %project.1.received_ref = f32[8,36,128]{2,1,0:T(8,128)} custom-call(s32[2,1,2,8]{3,2,1,0:T(2,128)} %bitcast.35, f32[32,128]{1,0:T(8,128)} %bitcast.34, f32[59,32,128]{2,1,0:T(8,128)} %bitcast.28), custom_call_target="tpu_custom_call" | custom-call | tf_op jit(solution)/shard_map/project/pallas_call | solution.py:100
  18.3 0.0 copy-done
  18.3 13.7 %render.1 = (f32[2,3,2,256]{3,2,1,0:T(2,128)}, f32[8,36,128]{2,1,0:T(8,128)}) custom-call(s32[2,2,8]{2,1,0:T(2,128)} %slot_ref.1, s32[2,2]{1,0:T(2,128)} %count_ref.1, f32[8,36,128]{2,1,0:T(8,128)} %project.1.received_ref, f32[2,3,2,256]{3,2,1,0:T(2,128)} %bitcast.39), custom_call_target="tpu_custom_call" | custom-call | flops 20000000000 | bytes 100000000 | tf_op jit(solution)/shard_map/render/pallas_call | solution.py:480
  32.0 17.3 %return_home.1.refs_3_ = f32[4,8,36,128]{3,2,1,0:T(8,128)} custom-call(f32[8,36,128]{2,1,0:T(8,128)} %get-tuple-element.12.x_ref), custom_call_target="tpu_custom_call" | custom-call | tf_op jit(solution)/shard_map/return_home/pallas_call | solution.py:224
  49.3 0.0 collective-permute-done.2.refs_8_
  49.3 0.0 copy-start.1
  49.3 0.0 collective-permute-done.1.refs_7_
  49.3 0.0 copy-start.2
  49.3 0.0 collective-permute-done.refs_6_
  49.4 0.0 copy-start.3
  49.4 0.7 %maximum_convert_fusion.refs_0_ = s32[4,128]{1,0:T(4,128)} fusion(f32[1,128]{1,0:T(1,128)S(1)} %slice.22, f32[1,128]{1,0:T(1,128)S(1)} %slice.21, f32[1,128]{1,0:T(1,128)S(1)} %slice.20, f32[1,128]{1,0:T(1,128)S(1)} %fusion), kind=kLoop, calls=%fused_computation.3 | loop fusion | flops 2048 | bytes 4096 | tf_op jit(solution)/shard_map/convert_element_type | solution.py:638
  50.1 0.0 copy-done.1
  50.1 0.2 copy-done.2
  50.2 0.2 copy-done.3
  50.5 5.1 %update.1 = (f32[59,32,128]{2,1,0:T(8,128)}, f32[59,8,128]{2,1,0:T(8,128)}, f32[59,8,128]{2,1,0:T(8,128)}, f32[8,60,128]{2,1,0:T(8,128)}) custom-call(s32[4,128]{1,0:T(4,128)} %maximum_convert_fusion.refs_0_, s32[1,8]{1,0:T(1,128)} %refs_1_.1, s32[1,8]{1,0:T(1,128)} %refs_2_.1, f32[4,8,36,128]{3,2,1,0:T(8,128)} %return_home.1.refs_3_, ...), custom_call_target="tpu_custom_call" | custom-call | tf_op jit(solution)/shard_map/update/pallas_call | solution.py:567
  55.5 10.6 %exchange_6.1.parent_ref = f32[8,60,128]{2,1,0:T(8,128)} custom-call(f32[8,60,128]{2,1,0:T(8,128)} %get-tuple-element.16.x_ref), custom_call_target="tpu_custom_call" | custom-call | tf_op jit(solution)/shard_map/exchange_6/pallas_call | solution.py:151
  66.1 2.0 %divide.1 = f32[8,59,2,128]{3,2,1,0:T(2,128)} custom-call(f32[8,60,128]{2,1,0:T(8,128)} %exchange_6.1.parent_ref), custom_call_target="tpu_custom_call" | custom-call | tf_op jit(solution)/shard_map/divide/pallas_call | solution.py:606
  (7 shorter events, 0.0 us)
Async XLA Ops:
  0.6 0.8 %copy-start.5 = (f32[2,9,59]{2,0,1:T(2,128)S(1)}, f32[2,9,59]{2,0,1:T(2,128)}, u32[]{:S(2)}) copy-start(f32[2,9,59]{2,0,1:T(2,128)} %param.13) | copy-start | bytes 12748
  1.4 1.1 %copy-start.4 = (f32[2,16,128]{2,1,0:T(8,128)}, f32[2,16,128]{2,1,0:T(8,128)S(1)}, u32[]{:S(2)}) copy-start(f32[2,16,128]{2,1,0:T(8,128)S(1)} %pad.8.clone) | copy-start | bytes 49156
  2.6 15.7 %copy-start = (f32[984,128]{1,0:T(8,128)}, f32[984,128]{1,0:T(8,128)S(1)}, u32[]{:S(2)}) copy-start(f32[984,128]{1,0:T(8,128)S(1)} %pad_maximum_fusion.refs_5_) | copy-start | bytes 1511428
  2.6 46.7 %collective-permute-start.2 = (f32[984,128]{1,0:T(8,128)S(1)}, f32[984,128]{1,0:T(8,128)S(1)}, u32[]{:S(2)}, u32[]{:S(2)}) collective-permute-start(f32[984,128]{1,0:T(8,128)S(1)} %pad_maximum_fusion.refs_5_), channel_id=1, source_target_pairs={{24,0},{0,8},{8,16},{16,24},{25,1},{1,9},{9,17},{17,25},{26,2},{2,... | collective-permute-start | bytes 1511432 | tf_op jit(solution)/shard_map/ppermute | solution.py:634
  4.7 44.7 %collective-permute-start.1 = (f32[984,128]{1,0:T(8,128)S(1)}, f32[984,128]{1,0:T(8,128)S(1)}, u32[]{:S(2)}, u32[]{:S(2)}) collective-permute-start(f32[984,128]{1,0:T(8,128)S(1)} %pad_maximum_fusion.refs_5_), channel_id=1, source_target_pairs={{16,0},{24,8},{0,16},{8,24},{17,1},{25,9},{1,17},{9,25},{18,2},{26... | collective-permute-start | bytes 1511432 | tf_op jit(solution)/shard_map/ppermute | solution.py:634
  5.9 43.5 %collective-permute-start = (f32[984,128]{1,0:T(8,128)S(1)}, f32[984,128]{1,0:T(8,128)S(1)}, u32[]{:S(2)}, u32[]{:S(2)}) collective-permute-start(f32[984,128]{1,0:T(8,128)S(1)} %pad_maximum_fusion.refs_5_), channel_id=1, source_target_pairs={{8,0},{16,8},{24,16},{0,24},{9,1},{17,9},{25,17},{1,25},{10,2},{18... | collective-permute-start | bytes 1511432 | tf_op jit(solution)/shard_map/ppermute | solution.py:634
  49.3 0.8 %copy-start.1 = (f32[984,128]{1,0:T(8,128)}, f32[984,128]{1,0:T(8,128)S(1)}, u32[]{:S(2)}) copy-start(f32[984,128]{1,0:T(8,128)S(1)} %collective-permute-done.2.refs_8_) | copy-start | bytes 1511428
  49.3 0.9 %copy-start.2 = (f32[984,128]{1,0:T(8,128)}, f32[984,128]{1,0:T(8,128)S(1)}, u32[]{:S(2)}) copy-start(f32[984,128]{1,0:T(8,128)S(1)} %collective-permute-done.1.refs_7_) | copy-start | bytes 1511428
  49.4 1.1 %copy-start.3 = (f32[984,128]{1,0:T(8,128)}, f32[984,128]{1,0:T(8,128)S(1)}, u32[]{:S(2)}) copy-start(f32[984,128]{1,0:T(8,128)S(1)} %collective-permute-done.refs_6_) | copy-start | bytes 1511428
